TPU v7x, 256 devices: a whole 4x4x8 slice. The times are simulated.
256 devices in a mesh: sub: 4 (over z_hi), row: 16 (over y, x), col: 4 (over z_lo, core).
Axes of the slice: x: 4, y: 4, z: 8 (z_hi: 4, z_lo: 2; z = z_hi * 2 + z_lo), core: 2. Of those that a mesh axis runs over, the one named last changes fastest.
Arguments:
- front_in: float32 [12288, 12288], P('row', ('sub', 'col')), as said below
- child_updates: float32 [4, 8192, 8192], P('sub', 'row', 'col'), as said below
- pattern: int32 [4, 32, 32], P('sub', 'row', 'col'), may hold values from 0 to 1, as said below
- child_map: int32 [4, 32], replicated, may hold values from 0 to 47, as said below
- pivot_inverse: float32 [1024, 1024], replicated, as said below
Outputs:
- front_out: float32 [12288, 12288], P('row', ('sub', 'col'))
Inputs may be any that keep to these rules, and one draw needn't show every extreme that they name: front_in is symmetric. Each child_updates[s] is symmetric. Each pattern[s] is symmetric. child_map[s] is strictly increasing, and child_map[s, i] // 3 equals i // 2. pivot_inverse is lower triangular with a positive diagonal.
All inputs are finite; a program needn't handle non-finite values.
Results may differ from a plain program's by a relative error of at most 0.000053.
Values sent between devices are 32-bit elements; how exact they have to be, the bound alone decides.
No kernel may reach another device: no remote copies, remote signals or barrier semaphores. Data moves between devices by JAX's collectives and lax.ppermute only.
A program may use at most 128 MiB of HBM per device.

v0:
```python
import jax
import jax.numpy as jnp
from jax import lax
from jax.sharding import PartitionSpec as P

BLK = 256
FRONT = 12288
CHILD = 8192
PANEL = 1024


def from_root(value, axis, source):
    kept = jnp.where(lax.axis_index(axis) == source, value, 0).astype(value.dtype)
    return lax.psum(kept, axis)


def times_transposed(left, right):
    return lax.dot_general(
        left,
        right,
        (((1,), (1,)), ((), ())),
        precision=lax.Precision.HIGHEST,
        preferred_element_type=jnp.float32,
    )


def shards(front_in, child_updates, pattern, child_map, pivot_inverse):
    sub_count = lax.axis_size("sub")
    row_count = lax.axis_size("row")
    col_count = lax.axis_size("col")
    groups = sub_count * col_count
    sub_id = lax.axis_index("sub")
    row_id = lax.axis_index("row")
    col_id = lax.axis_index("col")
    group_id = sub_id * col_count + col_id
    fblocks = FRONT // BLK
    cblocks = CHILD // BLK
    row_blocks = fblocks // row_count
    col_blocks = fblocks // groups
    child_rows = cblocks // row_count
    child_group = cblocks // groups
    child_cols = cblocks // col_count
    updates = child_updates[0].reshape(child_rows, BLK, child_cols, BLK)
    weights = pattern[0].astype(jnp.float32)
    masked = (updates * weights[:, None, :, None]).reshape(
        child_rows * BLK, sub_count, child_group * BLK
    )
    arrived = lax.all_to_all(
        lax.all_to_all(masked, "col", split_axis=1, concat_axis=1, tiled=True),
        "sub",
        split_axis=1,
        concat_axis=1,
        tiled=True,
    )
    rows_map = lax.dynamic_slice_in_dim(child_map, row_id * child_rows, child_rows, 1)
    cols_map = lax.dynamic_slice_in_dim(child_map, group_id * child_group, child_group, 1)
    row_targets = row_id * row_blocks + jnp.arange(row_blocks, dtype=jnp.int32)
    col_targets = group_id * col_blocks + jnp.arange(col_blocks, dtype=jnp.int32)
    row_hot = (rows_map[:, None, :] == row_targets[None, :, None]).astype(jnp.float32)
    col_hot = (cols_map[:, None, :] == col_targets[None, :, None]).astype(jnp.float32)
    pieces = arrived.reshape(child_rows, BLK, sub_count, child_group, BLK)
    spread_rows = jnp.einsum("spa,axsby->pxsby", row_hot, pieces, precision=lax.Precision.HIGHEST)
    extended = jnp.einsum("sqb,pxsby->pxqy", col_hot, spread_rows, precision=lax.Precision.HIGHEST)
    assembled = front_in + extended.reshape(row_blocks * BLK, col_blocks * BLK)
    panel_blocks = PANEL // BLK
    root_count = (panel_blocks + col_blocks - 1) // col_blocks
    gathered = []
    for owner in range(root_count):
        span_blocks = min(col_blocks, panel_blocks - owner * col_blocks)
        received_panel = from_root(assembled[:, : span_blocks * BLK], ("sub", "col"), owner)
        gathered.append(received_panel)
    panel_cols = jnp.concatenate(gathered, axis=1)
    factor = times_transposed(panel_cols, pivot_inverse)
    root_row = group_id * col_blocks // row_blocks
    column_factor = from_root(factor, "row", root_row)
    update = times_transposed(factor, column_factor)
    panel_parts = []
    for column in range(col_blocks):
        global_block = group_id * col_blocks + column
        panel_parts.append(
            lax.dynamic_slice_in_dim(
                factor, jnp.minimum(global_block, panel_blocks - 1) * BLK, BLK, 1
            )
        )
    panel_part = jnp.concatenate(panel_parts, axis=1)
    rows_global = (row_id * row_blocks * BLK + jnp.arange(row_blocks * BLK, dtype=jnp.int32)) // BLK
    cols_global = (
        group_id * col_blocks * BLK + jnp.arange(col_blocks * BLK, dtype=jnp.int32)
    ) // BLK
    below = (rows_global >= panel_blocks)[:, None]
    beyond = (cols_global >= panel_blocks)[None, :]
    result = jnp.where(below & beyond, assembled - update, jnp.where(below, panel_part, assembled))
    return result


def solution(mesh):
    in_specs = (P("row", ("sub", "col")), P("sub", "row", "col"), P("sub", "row", "col"), P(), P())
    out_specs = P("row", ("sub", "col"))
    return jax.shard_map(shards, mesh=mesh, in_specs=in_specs, out_specs=out_specs, check_vma=False)
```

profile of v0, /device:TPU:32, one launch (start us, length us, event | category | flops | bytes accessed | tf_op | source)
XLA Modules:
  0.0 482.4 jit_solution(3434529610521760695)
XLA Ops:
  6.5 0.7 convert_bitcast_fusion
  7.2 2.3 mul.52
  9.5 5.6 %mul.53 = f32[512,4,512]{2,1,0:T(4,128)} reshape(f32[2,256,8,256]{3,2,1,0:T(8,128)} %mul.52) | data formatting | bytes 8388608 | tf_op jit(solution)/shard_map/mul | solution.py:45
  15.2 5.3 %copy.11 = f32[512,4,512]{0,2,1:T(8,128)} copy(f32[512,4,512]{2,1,0:T(4,128)} %mul.53) | data formatting | bytes 8388608 | tf_op jit(solution)/shard_map/mul | solution.py:45
  20.4 5.4 %copy.10 = f32[1,512,2048]{1,2,0:T(8,128)} copy(f32[1,512,2048]{2,1,0:T(8,128)} %param.6) | data formatting | bytes 8388608 | tf_op args[1]
  25.8 6.4 %mul.54 = f32[512,4,512]{0,2,1:T(8,128)} multiply(f32[512,4,512]{0,2,1:T(8,128)} %bitcast.29, f32[512,4,512]{0,2,1:T(8,128)} %copy.11) | non-fusion elementwise | flops 1048576 | bytes 12582912 | tf_op jit(solution)/shard_map/mul | solution.py:45
  32.2 5.2 %copy.12 = f32[512,4,512]{2,0,1:T(8,128)} copy(f32[512,4,512]{0,2,1:T(8,128)} %mul.54) | data formatting | bytes 8388608 | tf_op jit(solution)/shard_map/mul | solution.py:45
  37.5 54.0 %all_to_all.10 = f32[512,4,512]{2,0,1:T(8,128)} all-to-all(f32[512,4,512]{2,0,1:T(8,128)} %copy.12), channel_id=1, replica_groups=mesh['sub'=4,'row'=16,'col'=4] {'col'}, dimensions={1} | all-to-all | bytes 8388608 | tf_op jit(solution)/shard_map/all_to_all | solution.py:49
  91.5 0.0 copy-start.2
  91.5 6.9 %all-to-all-start.1 = ((f32[512,4,512]{2,0,1:T(8,128)}), f32[512,4,512]{2,0,1:T(8,128)}, u32[]{:S(2)}, u32[]{:S(2)}) async-start(f32[512,4,512]{2,0,1:T(8,128)} %all_to_all.10), calls=%async_computation.1 | async-start | bytes 8388608 | tf_op jit(solution)/shard_map/all_to_all | solution.py:48
  98.4 0.0 all-reduce.6.cloned.1.call-start
  98.4 0.0 copy-done.2
  98.4 0.1 constant_dynamic-slice_fusion.3
  98.4 0.1 copy.14
  98.5 89.9 %all-to-all-done.1 = f32[512,4,512]{2,0,1:T(8,128)} async-done(((f32[512,4,512]{2,0,1:T(8,128)}), f32[512,4,512]{2,0,1:T(8,128)}, u32[]{:S(2)}, u32[]{:S(2)}) %all-to-all-start.1) | async-done | bytes 4194336 | tf_op jit(solution)/shard_map/all_to_all | solution.py:48
  188.5 5.9 %reshape.65 = f32[2,256,4,2,256]{4,3,1,0,2:T(2,128)} reshape(f32[512,4,512]{2,0,1:T(8,128)} %all-to-all-done.1) | data formatting | bytes 8388608 | tf_op jit(solution)/shard_map/reshape | solution.py:61
  194.4 13.8 %convolution_bitcast_fusion = f32[3,256,4,2,256]{4,0,3,1,2:T(4,128)S(1)} fusion(f32[2,256,4,2,256]{4,3,1,0,2:T(2,128)} %reshape.65, s32[3]{0:T(128)S(1)} %iota_add_fusion.3, s32[4,2]{1,0:T(4,128)S(1)} %get-tuple-element.13), kind=kOutput, calls=%fused_computation.2 | convolution fusion | flops 37748760 | bytes 10485804 | tf_op jit(solution)/shard_map/spa,axsby->pxsby/dot_general | solution.py:62
  208.1 7.4 %fusion = f32[3,256,256,3,1]{2,3,4,1,0:T(4,128)S(1)} fusion(f32[3,256,4,2,256]{4,0,3,1,2:T(4,128)S(1)} %convolution_bitcast_fusion, s32[4,2]{0,1:T(2,128)S(1)} %copy.14, s32[3]{0:T(128)S(1)} %iota_add_fusion.2), kind=kOutput, calls=%fused_computation | convolution fusion | flops 56623128 | bytes 8650796 | tf_op jit(solution)/shard_map/sqb,pxsby->pxqy/dot_general | solution.py:63
  215.6 0.0 copy-start.1
  215.6 0.6 copy.19
  216.2 1.1 copy-done.1
  217.2 1.7 broadcast_select_fusion.1
  219.0 0.0 copy-start
  219.0 1.5 copy-done
  220.4 0.9 slice_select_fusion
  221.4 0.0 all-reduce.6.cloned.1.call-update
  221.4 0.3 all-reduce.4.cloned.1.call-start
  221.7 118.6 %all-reduce.6.cloned.1.call-done = (f32[768,256]{1,0:T(8,128)}, f32[768,768]{1,0:T(8,128)}) async-done(((f32[768,256]{1,0:T(8,128)}, f32[768,768]{1,0:T(8,128)}), (f32[768,256]{1,0:T(8,128)}, f32[768,768]{1,0:T(8,128)})) %all-reduce.6.cloned.1.call-update) | async-done | bytes 3145744 | tf_op jit(solution)/shard_map/psum | solution.py:14
  340.3 14.4 %broadcast_select_fusion = (f32[768,1024]{1,0:T(8,128)}, f32[768,1024]{1,0:T(8,128)S(1)}) fusion(pred[]{:T(512)S(6)} %eq.43, f32[1024,1024]{1,0:T(8,128)} %param.9, f32[768,256]{1,0:T(8,128)} %get-tuple-element.5, f32[768,768]{1,0:T(8,128)} %get-tuple-element.6), kind=kOutput, calls=%fused_computation.10 | convolution fusion | flops 9665249280 | bytes 13631489 | tf_op jit(solution)/shard_map/dot_general | solution.py:18
  354.7 0.0 all-reduce.4.cloned.1.call-update
  354.7 1.6 constant_dynamic-slice_fusion.2
  356.3 107.3 %all-reduce.4.cloned.1.call-done = f32[768,1024]{1,0:T(8,128)} async-done(((f32[768,1024]{1,0:T(8,128)}), f32[768,1024]{1,0:T(8,128)}) %all-reduce.4.cloned.1.call-update) | async-done | bytes 3145744 | tf_op jit(solution)/shard_map/psum | solution.py:14
  463.7 11.9 %fusion.7 = f32[768,768]{1,0:T(8,128)} fusion(f32[768,768]{1,0:T(8,128)} %copy-done, f32[768,256]{1,0:T(8,128)} %get-tuple-element.10, f32[768,256]{1,0:T(8,128)} %get-tuple-element.11, f32[768,256]{1,0:T(8,128)} %get-tuple-element.9, f32[768,1024]{1,0:T(8,128)S(1)} %get-tuple-element.15, f32[768,1024]{1,0:T(8,128)} %all-reduce.4.cloned.1.call-done, ...), kind=kOutput, calls=%fused_computation.9 | convolution fusion | flops 7251296256 | bytes 13370880 | tf_op jit(solution)/shard_map/dot_general | solution.py:18
  (3 shorter events, 0.0 us)
Async XLA Ops:
  91.5 6.9 %copy-start.2 = (s32[4,32]{1,0:T(4,128)S(1)}, s32[4,32]{1,0:T(4,128)}, u32[]{:S(2)}) copy-start(s32[4,32]{1,0:T(4,128)} %param.8) | copy-start | bytes 1540
  91.5 96.9 %all-to-all-start.1 = ((f32[512,4,512]{2,0,1:T(8,128)}), f32[512,4,512]{2,0,1:T(8,128)}, u32[]{:S(2)}, u32[]{:S(2)}) async-start(f32[512,4,512]{2,0,1:T(8,128)} %all_to_all.10), calls=%async_computation.1 | async-start | bytes 8388608 | tf_op jit(solution)/shard_map/all_to_all | solution.py:48
  98.4 241.9 %all-reduce.6.cloned.1.call-start = ((), (), s32[]{:S(2)}) async-start(), calls=%async_computation.3 | async-start | bytes 6291456 | tf_op jit(solution)/shard_map/psum | solution.py:14
  215.6 1.7 copy-start.1
  219.0 1.5 copy-start
  221.4 242.3 %all-reduce.4.cloned.1.call-start = ((), (), s32[]{:S(2)}) async-start(), calls=%async_computation.2 | async-start | bytes 6291456 | tf_op jit(solution)/shard_map/psum | solution.py:14
Sparse Core Ops, SparseCore 0:
  221.5 118.7 all-reduce.5
  354.8 108.8 all-reduce.3
where the time goes:
time: 484 us; the launch traced here: 482 us
  waiting for transfers between devices  316 us (65%)
  blocking collectives  54 us (11%)
  matrix products  47.5 us (10%)
  local copies, waits for them, and re-layouts  34.6 us (7%)
  between operations  13.5 us (3%)
  other arithmetic  9.79 us (2%)
  starting transfers between devices  7.12 us (1%)
    psum x2, waiting for transfers between devices, from_root(): return lax.psum(kept, axis)  226 us
    all_to_all x1, waiting for transfers between devices, shards(): lax.all_to_all(lax.all_to_all(masked, 'col', split_axis=1, concat_axis=1,...  89.9 us
    all_to_all x1, blocking collectives, shards(): lax.all_to_all(masked, 'col', split_axis=1, concat_axis=1, tiled=True)  54 us
    dot_general x2, matrix products, times_transposed(): lax.dot_general(left, right, (((1,), (1,)), ((), ())), precision=lax.Prec...  26.3 us
    mul x4, local copies, waits for them, and re-layouts, shards(): updates * weights[:, None, :, None]  18.5 us
    dot_general x1, matrix products, shards(): jnp.einsum('spa,axsby->pxsby', row_hot, pieces, precision=lax.Precision.H...  13.8 us
  transfers between devices with their start and end apart: 3, of which 3 were waited for; matrix products, arithmetic and copies ran while one was open for 0% of the time, Pallas kernels for 0%

commit v1 on v0

v1 whole, which is shorter than its diff:
```python
import jax
import jax.numpy as jnp
from jax import lax
from jax.experimental import pallas as pl
from jax.experimental.pallas import tpu as pltpu
from jax.sharding import PartitionSpec as P

BLK = 256
PANEL = 1024
RING = ("sub", "col")
MESH = ("sub", "row", "col")
SMEM = pl.BlockSpec(memory_space=pltpu.SMEM)
VMEM = pl.BlockSpec(memory_space=pltpu.VMEM)
PARAMS = pltpu.CompilerParams(vmem_limit_bytes=56 * 1024 * 1024)
F32 = jnp.float32


def split(x):
    hi = x.astype(jnp.bfloat16)
    return hi, (x - hi.astype(F32)).astype(jnp.bfloat16)


def times_transposed(left, right):
    lh, ll = split(left)
    rh, rl = split(right)

    def dot(a, b):
        return lax.dot_general(a, b, (((1,), (1,)), ((), ())), preferred_element_type=F32)

    return dot(lh, rl) + dot(ll, rh) + dot(lh, rh)


def place(cmap, child, group, slot):
    target = 3 * group + slot
    first = (cmap[child, 2 * group] == target).astype(jnp.int32)
    second = (cmap[child, 2 * group + 1] == target).astype(jnp.int32)
    return second, first + second


def mask_kernel(ids, pat, *refs):
    i = pl.program_id(0)
    for j in range(4):
        group = (ids[0] + j) % 4
        for b in range(2):
            cols = pl.ds(b * BLK, BLK)
            refs[4 + j][:, cols] = refs[j][0, :, cols] * pat[i, 2 * group + b].astype(F32)


def masked_groups(ids, pat, child):
    def group(j):
        return pl.BlockSpec((1, BLK, 2 * BLK), lambda i, ids, pat: (0, i, (ids[0] + j) % 4))

    return pl.pallas_call(
        mask_kernel,
        grid_spec=pltpu.PrefetchScalarGridSpec(
            num_scalar_prefetch=2,
            grid=(2,),
            in_specs=[group(j) for j in range(4)],
            out_specs=[pl.BlockSpec((BLK, 2 * BLK), lambda i, ids, pat: (i, 0))] * 4,
        ),
        out_shape=[jax.ShapeDtypeStruct((2 * BLK, 2 * BLK), F32)] * 4,
        compiler_params=PARAMS,
        name="masked_groups",
    )(ids, pat, child, child, child, child)


def panel_kernel(ids, pat, cmap, child, front, last, *outs):
    s = ids[0]
    row = ids[1]
    root = (s == 0).astype(F32)
    cols = [place(cmap, s, 0, q) for q in range(3)]
    cols.append((jnp.int32(2), (cmap[s, 2] == 3).astype(jnp.int32)))
    for p in range(3):
        a, a_ok = place(cmap, s, row, p)
        for q in range(4):
            b, b_ok = cols[q]
            weight = (pat[a, b] * a_ok * b_ok).astype(F32)
            for d in range(8):
                z = (2 * s + d) % 8
                src = pl.multiple_of(a * BLK + z * 32, 32)
                own = pl.ds(pl.multiple_of(p * BLK + z * 32, 32), 32)
                value = child[0, pl.ds(src, 32), pl.ds(pl.multiple_of(b * BLK, BLK), BLK)] * weight
                kept = front[own, pl.ds(q * BLK, BLK)] if q < 3 else last[own, :]
                outs[d][p, :, pl.ds(q * BLK, BLK)] = value + kept * root


def panel_slices(ids, pat, cmap, child, front, last):
    return pl.pallas_call(
        panel_kernel,
        grid=(1,),
        in_specs=[
            SMEM,
            SMEM,
            SMEM,
            pl.BlockSpec((1, 2 * BLK, 3 * BLK), lambda i: (0, 0, 0)),
            pl.BlockSpec((3 * BLK, 3 * BLK), lambda i: (0, 0)),
            pl.BlockSpec((3 * BLK, BLK), lambda i: (0, 0)),
        ],
        out_specs=[pl.BlockSpec((3, 32, PANEL), lambda i: (0, 0, 0))] * 8,
        out_shape=[jax.ShapeDtypeStruct((3, 32, PANEL), F32)] * 8,
        compiler_params=PARAMS,
        name="panel_slices",
    )(ids, pat, cmap, child, front, last)


def factor_kernel(ids, *refs):
    parts, pivot, out = refs[:8], refs[8], refs[9]
    odd = (2 * ids[0] + ids[2] // 2) % 2

    def total(which):
        value = parts[which][...]
        for m in range(1, 4):
            value = value + parts[which + 2 * m][...]
        return value.reshape(96, PANEL)

    rows = jnp.where(odd == 1, total(1), total(0))
    out[...] = times_transposed(rows, pivot[...]).reshape(3, 32, PANEL)


def factor_slice(ids, parts, pivot):
    return pl.pallas_call(
        factor_kernel,
        in_specs=[SMEM] + [VMEM] * 9,
        out_specs=VMEM,
        out_shape=jax.ShapeDtypeStruct((3, 32, PANEL), F32),
        compiler_params=PARAMS,
        name="factor_slice",
    )(ids, *parts, pivot)


def final_kernel(ids, cmap, front, r0, r1, r2, r3, left, right, out):
    p = pl.program_id(0)
    q = pl.program_id(1)
    row = ids[1]
    group = 4 * ids[0] + ids[2]
    value = front[...]
    for j, ref in enumerate((r0, r1, r2, r3)):
        child = (ids[2] - j + 4) % 4
        ok = place(cmap, child, row, p)[1] * place(cmap, child, group, q)[1]
        value = value + ref[...] * ok.astype(F32)
    row_block = 3 * row + p
    col_block = 3 * group + q
    out[...] = value

    @pl.when((row_block >= 4) & (col_block < 4))
    def _():
        cols = pl.ds(pl.multiple_of(jnp.minimum(col_block, 3) * BLK, BLK), BLK)
        out[...] = left[:, 0, :, cols].reshape(BLK, BLK)

    @pl.when((row_block >= 4) & (col_block >= 4))
    def _():
        out[...] = value - times_transposed(left[...].reshape(BLK, PANEL), right[...].reshape(BLK, PANEL))


def final(ids, cmap, front, arrived, left, right):
    def from_child(j):
        def where(p, q, ids, cmap):
            child = (ids[2] - j + 4) % 4
            return (
                place(cmap, child, ids[1], p)[0],
                place(cmap, child, 4 * ids[0] + ids[2], q)[0],
            )

        return pl.BlockSpec((BLK, BLK), where)

    tile = pl.BlockSpec((BLK, BLK), lambda p, q, ids, cmap: (p, q))
    return pl.pallas_call(
        final_kernel,
        grid_spec=pltpu.PrefetchScalarGridSpec(
            num_scalar_prefetch=2,
            grid=(3, 3),
            in_specs=[tile]
            + [from_child(j) for j in range(4)]
            + [
                pl.BlockSpec((8, 1, 32, PANEL), lambda p, q, ids, cmap: (0, p, 0, 0)),
                pl.BlockSpec((16, 1, 16, PANEL), lambda p, q, ids, cmap: (0, q, 0, 0)),
            ],
            out_specs=tile,
        ),
        out_shape=jax.ShapeDtypeStruct((3 * BLK, 3 * BLK), F32),
        compiler_params=PARAMS,
        name="final",
    )(ids, cmap, front, *arrived, left, right)


def shards(front_in, child_updates, pattern, child_map, pivot_inverse):
    sub = lax.axis_index("sub")
    row = lax.axis_index("row")
    col = lax.axis_index("col")
    ids = jnp.stack([sub, row, col]).astype(jnp.int32)
    core = col % 2
    z = 2 * sub + col // 2
    pat = pattern[0]

    last = lax.ppermute(front_in[:, :BLK], RING, [(1, 0)])
    slices = panel_slices(ids, pat, child_map, child_updates, front_in, last)
    parts = [slices[0]]
    for d in range(1, 8):
        parts.append(lax.ppermute(slices[d], RING, [(4 * s, 2 * ((2 * s + d) % 8)) for s in range(4)]))

    sent = masked_groups(ids, pat, child_updates)
    arrived = [
        lax.ppermute(
            sent[j], RING, [(4 * s + c, 4 * c + (s + j) % 4) for s in range(4) for c in range(4)]
        )
        for j in range(4)
    ]

    mine = factor_slice(ids, parts, pivot_inverse)
    other = lax.ppermute(mine, RING, [(2 * k, 2 * k + 1) for k in range(8)])
    mine = jnp.where(core == 0, mine, other)

    half = lax.dynamic_slice_in_dim(mine, core * 16, 16, 1)
    turn = [
        ((s * 16 + r) * 4 + c, ((r // 4) * 16 + 4 * s + c) * 4 + r % 4)
        for s in range(4)
        for r in range(16)
        for c in range(4)
    ]
    right = lax.all_gather(lax.ppermute(half, MESH, turn), "row", axis=0)

    onward = [(2 * k, 2 * ((k + 1) % 8)) for k in range(8)]
    onward += [(2 * k + 1, 2 * ((k - 1) % 8) + 1) for k in range(8)]
    swap = [(k, k ^ 1) for k in range(16)]
    step = 1 - 2 * core
    left = jnp.zeros((8,) + mine.shape, F32)
    left = lax.dynamic_update_slice_in_dim(left, mine[None], z, 0)
    piece = mine
    for t in range(1, 5):
        piece = lax.ppermute(piece, RING, onward)
        left = lax.dynamic_update_slice_in_dim(left, piece[None], (z - t * step) % 8, 0)
        if t < 4:
            swapped = lax.ppermute(piece, RING, swap)
            left = lax.dynamic_update_slice_in_dim(left, swapped[None], (z + t * step) % 8, 0)
    return final(ids, child_map, front_in, arrived, left, right)


def solution(mesh):
    in_specs = (P("row", ("sub", "col")), P("sub", "row", "col"), P("sub", "row", "col"), P(), P())
    out_specs = P("row", ("sub", "col"))
    return jax.shard_map(shards, mesh=mesh, in_specs=in_specs, out_specs=out_specs, check_vma=False)
```

time: 484 us -> 258 us (0.53)
  waiting for transfers between devices: 316 us -> 133 us
  starting transfers between devices: 7.12 us -> 74.5 us
  blocking collectives: 54 us -> 0 us
  matrix products: 47.5 us -> 0 us
  Pallas kernels: 0 us -> 26.6 us
  local copies, waits for them, and re-layouts: 34.6 us -> 8.48 us
  other arithmetic: 9.79 us -> 0.73 us
    psum x2 -> x0, waiting for transfers between devices: 226 us -> none  [from_root(): return lax.psum(kept, axis)]
    ppermute x0 -> x21, waiting for transfers between devices: none -> 133 us  [the longest x4 87.8 us: shards(): piece = lax.ppermute(piece, RING, onward)]
    all_to_all x1 -> x0, waiting for transfers between devices: 89.9 us -> none  [shards(): lax.all_to_all(lax.all_to_all(masked, 'col', split_axis=1, concat_axis=1,...]
    ppermute x0 -> x21, starting transfers between devices: none -> 74.5 us  [the longest x3 43.1 us: shards(): swapped = lax.ppermute(piece, RING, swap)]
    all_to_all x1 -> x0, blocking collectives: 54 us -> none  [shards(): lax.all_to_all(masked, 'col', split_axis=1, concat_axis=1, tiled=True)]
    dot_general x4 -> x0, matrix products: 47.5 us -> none  [the longest x2 26.3 us: times_transposed(): lax.dot_general(left, right, (((1,), (1,)), ((), ())), precision=lax.Prec...]
    pallas_call x0 -> x4, Pallas kernels: none -> 26.6 us  [the longest x1 11.8 us: final(): pl.pallas_call(final_kernel, grid_spec=pltpu.PrefetchScalarGridSpec(num_s...]
    mul x4 -> x0, local copies, waits for them, and re-layouts: 18.5 us -> none  [shards(): updates * weights[:, None, :, None]]
  transfers between devices with their start and end apart: 3 -> 22, of which waited for: 3 -> 10; matrix products, arithmetic and copies ran while one was open for 0% -> 1% of each run, Pallas kernels for 0% -> 2%
where the time goes in v1:
time: 258 us; the launch traced here: 257 us
  waiting for transfers between devices  133 us (52%)
  starting transfers between devices  74.5 us (29%)
  Pallas kernels  26.6 us (10%)
  between operations  13.9 us (5%)
  local copies, waits for them, and re-layouts  8.48 us (3%)
    ppermute x4, waiting for transfers between devices, shards(): piece = lax.ppermute(piece, RING, onward)  87.8 us
    ppermute x3, starting transfers between devices, shards(): swapped = lax.ppermute(piece, RING, swap)  43.1 us
    ppermute x7, waiting for transfers between devices, shards(): lax.ppermute(slices[d], RING, [(4 * s, 2 * ((2 * s + d) % 8)) for s in ra...  28.7 us
    ppermute x1, waiting for transfers between devices, shards(): right = lax.all_gather(lax.ppermute(half, MESH, turn), 'row', axis=0)  14 us
    ppermute x4, starting transfers between devices, shards(): lax.ppermute(sent[j], RING, [(4 * s + c, 4 * c + (s + j) % 4) for s in ra...  13.2 us
    pallas_call x1, Pallas kernels, final(): pl.pallas_call(final_kernel, grid_spec=pltpu.PrefetchScalarGridSpec(num_s...  11.8 us
    ppermute x7, starting transfers between devices, shards(): lax.ppermute(slices[d], RING, [(4 * s, 2 * ((2 * s + d) % 8)) for s in ra...  7.2 us
    pallas_call x1, Pallas kernels, factor_slice(): pl.pallas_call(factor_kernel, in_specs=[SMEM] + [VMEM] * 9, out_specs=VME...  6.02 us
  transfers between devices with their start and end apart: 22, of which 10 were waited for; matrix products, arithmetic and copies ran while one was open for 1% of the time, Pallas kernels for 2%

profile of v1, /device:TPU:32, one launch (start us, length us, event | category | flops | bytes accessed | tf_op | source)
XLA Modules:
  0.0 256.8 jit_solution(14494709925513213077)
XLA Ops:
  6.5 1.2 slice.3
  7.7 0.7 collective-permute-start.4
  8.4 0.7 pad_add_fusion.ids
  9.1 0.0 collective-permute-done.4.last
  9.1 0.9 copy-done.3
  10.0 4.3 %panel_slices.1 = (f32[3,32,1024]{2,1,0:T(8,128)}, f32[3,32,1024]{2,1,0:T(8,128)}, f32[3,32,1024]{2,1,0:T(8,128)}, f32[3,32,1024]{2,1,0:T(8,128)}, f32[3,32,1024...) custom-call(s32[3]{0:T(128)} %pad_add_fusion.ids, s32[2,8]{1,0:T(2,128)} %bitcast.22, ...), custom_call_target="tpu_custom_call" | custom-call | tf_op jit(solution)/shard_map/panel_slices/pallas_call | solution.py:88
  14.3 1.3 collective-permute-start.5
  15.6 0.7 collective-permute-start.6
  16.3 1.3 collective-permute-start.7
  17.6 0.7 collective-permute-start.8
  18.3 1.3 collective-permute-start.9
  19.6 6.6 %collective-permute-done.5.refs_1_ = f32[3,32,1024]{2,1,0:T(8,128)S(1)} collective-permute-done((f32[3,32,1024]{2,1,0:T(8,128)}, f32[3,32,1024]{2,1,0:T(8,128)S(1)}, u32[]{:S(2)}, u32[]{:S(2)}) %collective-permute-start.5) | collective-permute-done | bytes 393248 | tf_op jit(solution)/shard_map/ppermute | solution.py:199
  26.2 0.7 collective-permute-start.10
  26.9 1.3 collective-permute-start.11
  28.2 17.7 %collective-permute-done.7.refs_3_ = f32[3,32,1024]{2,1,0:T(8,128)S(1)} collective-permute-done((f32[3,32,1024]{2,1,0:T(8,128)}, f32[3,32,1024]{2,1,0:T(8,128)S(1)}, u32[]{:S(2)}, u32[]{:S(2)}) %collective-permute-start.7) | collective-permute-done | bytes 393248 | tf_op jit(solution)/shard_map/ppermute | solution.py:199
  45.9 4.4 %collective-permute-done.11.refs_7_ = f32[3,32,1024]{2,1,0:T(8,128)S(1)} collective-permute-done((f32[3,32,1024]{2,1,0:T(8,128)}, f32[3,32,1024]{2,1,0:T(8,128)S(1)}, u32[]{:S(2)}, u32[]{:S(2)}) %collective-permute-start.11) | collective-permute-done | bytes 393248 | tf_op jit(solution)/shard_map/ppermute | solution.py:199
  50.4 0.7 copy-done.10
  51.1 6.0 %factor_slice.1 = f32[3,32,1024]{2,1,0:T(8,128)} custom-call(s32[3]{0:T(128)} %pad_add_fusion.ids, f32[3,32,1024]{2,1,0:T(8,128)} %get-tuple-element.21.refs_0_, f32[3,32,1024]{2,1,0:T(8,128)} %copy-done.4, f32[3,32,1024]{2,1,0:T(8,128)} %copy-done.5, f32[3,32,1024]{2,1,0:T(8,128)} %copy-done.6, f32[3,32,1024]{2,1,0:T(8,128)} %copy-done.7, ...), custom_call_target="tpu_custom_call" | custom-call | tf_op jit(solution)/shard_map/factor_slice/pallas_call | solution.py:121
  57.1 2.2 collective-permute-start.12
  59.3 0.9 collective-permute-done.12
  60.2 0.4 broadcast_in_dim.27
  60.6 0.1 bitcast_dynamic-update-slice_fusion.7
  60.7 0.0 copy-start.2
  60.7 0.7 copy-done.2
  61.4 4.2 %collective-permute-start.20 = (f32[3,16,1024]{2,1,0:T(8,128)S(1)}, f32[3,16,1024]{2,1,0:T(8,128)S(1)}, u32[]{:S(2)}, u32[]{:S(2)}) collective-permute-start(f32[3,16,1024]{2,1,0:T(8,128)S(1)} %constant_dynamic-slice_fusion), channel_id=1, source_target_pairs={{0,0},{1,4},{2,8},{3,12},{4,1},{5,5},{6,9},{7,13},{8,2},{9,6},{10,... | collective-permute-start | bytes 589832 | tf_op jit(solution)/shard_map/ppermute | solution.py:220
  65.6 14.0 %collective-permute-done.20 = f32[3,16,1024]{2,1,0:T(8,128)S(1)} collective-permute-done((f32[3,16,1024]{2,1,0:T(8,128)S(1)}, f32[3,16,1024]{2,1,0:T(8,128)S(1)}, u32[]{:S(2)}, u32[]{:S(2)}) %collective-permute-start.20) | collective-permute-done | bytes 196640 | tf_op jit(solution)/shard_map/ppermute | solution.py:220
  79.6 0.7 copy-done.11
  80.3 0.0 all-gather.3.cloned.1.call-update
  80.3 0.1 collective-permute-start.13
  80.4 8.1 %collective-permute-done.13 = f32[3,32,1024]{2,1,0:T(8,128)} collective-permute-done((f32[3,32,1024]{2,1,0:T(8,128)}, f32[3,32,1024]{2,1,0:T(8,128)}, u32[]{:S(2)}, u32[]{:S(2)}) %collective-permute-start.13) | collective-permute-done | bytes 393248 | tf_op jit(solution)/shard_map/ppermute | solution.py:230
  88.5 0.0 collective-permute-start.15
  88.5 12.5 %collective-permute-start.14 = (f32[3,32,1024]{2,1,0:T(8,128)}, f32[3,32,1024]{2,1,0:T(8,128)}, u32[]{:S(2)}, u32[]{:S(2)}) collective-permute-start(f32[3,32,1024]{2,1,0:T(8,128)} %collective-permute-done.13), channel_id=1, source_target_pairs={{0,1},{1,0},{2,3},{3,2},{64,65},{65,64},{66,67},{67,66},{128,129},... | collective-permute-start | bytes 1179656 | tf_op jit(solution)/shard_map/ppermute | solution.py:233
  101.0 4.5 %masked_groups.1 = (f32[512,512]{1,0:T(8,128)}, f32[512,512]{1,0:T(8,128)}, f32[512,512]{1,0:T(8,128)}, f32[512,512]{1,0:T(8,128)}) custom-call(s32[3]{0:T(128)} %pad_add_fusion.ids, s32[2,8]{1,0:T(2,128)} %bitcast.23, f32[1,512,2048]{2,1,0:T(8,128)} %child.1, f32[1,512,2048]{2,1,0:T(8,128)} %child.1, f32[1,512,2048]{2,1,0:T(8,128)} %child.1, ...), custom_call_target="tpu_custom_call" | custom-call | tf_op jit(solution)/shard_map/masked_groups/pallas_call | solution.py:53
  105.4 1.9 collective-permute-start
  107.3 0.1 collective-permute-start.1
  107.6 0.7 collective-permute-done.15
  108.3 3.8 %collective-permute-start.17 = (f32[3,32,1024]{2,1,0:T(8,128)S(1)}, f32[3,32,1024]{2,1,0:T(8,128)S(1)}, u32[]{:S(2)}, u32[]{:S(2)}) collective-permute-start(f32[3,32,1024]{2,1,0:T(8,128)S(1)} %collective-permute-done.15), channel_id=1, source_target_pairs={{0,2},{2,64},{64,66},{66,128},{128,130},{130,192},{192,194},{194,0... | collective-permute-start | bytes 1179656 | tf_op jit(solution)/shard_map/ppermute | solution.py:230
  112.1 0.1 collective-permute-start.16
  112.1 1.0 bitcast_dynamic-update-slice_fusion.6
  113.2 11.2 %collective-permute-start.2 = (f32[512,512]{1,0:T(8,128)}, f32[512,512]{1,0:T(8,128)}, u32[]{:S(2)}, u32[]{:S(2)}) collective-permute-start(f32[512,512]{1,0:T(8,128)} %get-tuple-element.19), channel_id=1, source_target_pairs={{0,2},{1,66},{2,130},{3,194},{64,3},{65,67},{66,131},{67,195},{128... | collective-permute-start | bytes 3145736 | tf_op jit(solution)/shard_map/ppermute | solution.py:203
  124.4 1.1 bitcast_dynamic-update-slice_fusion.5
  125.5 39.3 %collective-permute-done.17 = f32[3,32,1024]{2,1,0:T(8,128)S(1)} collective-permute-done((f32[3,32,1024]{2,1,0:T(8,128)S(1)}, f32[3,32,1024]{2,1,0:T(8,128)S(1)}, u32[]{:S(2)}, u32[]{:S(2)}) %collective-permute-start.17) | collective-permute-done | bytes 393248 | tf_op jit(solution)/shard_map/ppermute | solution.py:230
  164.8 30.5 %collective-permute-start.18 = (f32[3,32,1024]{2,1,0:T(8,128)S(1)}, f32[3,32,1024]{2,1,0:T(8,128)S(1)}, u32[]{:S(2)}, u32[]{:S(2)}) collective-permute-start(f32[3,32,1024]{2,1,0:T(8,128)S(1)} %collective-permute-done.17), channel_id=1, source_target_pairs={{0,1},{1,0},{2,3},{3,2},{64,65},{65,64},{66,67},{67,66},{128,129},... | collective-permute-start | bytes 1179656 | tf_op jit(solution)/shard_map/ppermute | solution.py:233
  195.4 1.3 collective-permute-done.18
  196.7 39.7 %collective-permute-done.19 = f32[3,32,1024]{2,1,0:T(8,128)S(1)} collective-permute-done((f32[3,32,1024]{2,1,0:T(8,128)S(1)}, f32[3,32,1024]{2,1,0:T(8,128)S(1)}, u32[]{:S(2)}, u32[]{:S(2)}) %collective-permute-start.19) | collective-permute-done | bytes 393248 | tf_op jit(solution)/shard_map/ppermute | solution.py:230
  236.6 0.0 all-gather.3.cloned.1.call-done
  236.6 1.6 copy-done
  238.2 11.8 %final.1 = f32[768,768]{1,0:T(8,128)} custom-call(s32[3]{0:T(128)} %pad_add_fusion.ids, s32[4,32]{1,0:T(4,128)} %cmap.3, f32[768,768]{1,0:T(8,128)} %front.3, f32[512,512]{1,0:T(8,128)} %collective-permute-done.r0, f32[512,512]{1,0:T(8,128)} %collective-permute-done.1.r1, f32[512,512]{1,0:T(8,128)} %collective-permute-done.2.r2, ...), custom_call_target="tpu_custom_call" | custom-call | tf_op jit(solution)/shard_map/final/pallas_call | solution.py:167
  (37 shorter events, 0.2 us)
Async XLA Ops:
  6.5 230.0 %all-gather.3.cloned.1.call-start = ((), (), s32[]{:S(2)}) async-start(), calls=%async_computation | async-start | bytes 3342336 | tf_op jit(solution)/shard_map/all_gather | solution.py:220
  7.7 1.4 collective-permute-start.4
  9.1 0.9 copy-start.3
  14.3 11.9 %collective-permute-start.5 = (f32[3,32,1024]{2,1,0:T(8,128)}, f32[3,32,1024]{2,1,0:T(8,128)S(1)}, u32[]{:S(2)}, u32[]{:S(2)}) collective-permute-start(f32[3,32,1024]{2,1,0:T(8,128)} %get-tuple-element.22), channel_id=1, source_target_pairs={{0,2},{64,66},{128,130},{192,194},{4,6},{68,70},{132,134},{196,198... | collective-permute-start | bytes 1179656 | tf_op jit(solution)/shard_map/ppermute | solution.py:199
  15.6 11.3 %collective-permute-start.6 = (f32[3,32,1024]{2,1,0:T(8,128)}, f32[3,32,1024]{2,1,0:T(8,128)S(1)}, u32[]{:S(2)}, u32[]{:S(2)}) collective-permute-start(f32[3,32,1024]{2,1,0:T(8,128)} %get-tuple-element.23), channel_id=1, source_target_pairs={{0,64},{64,128},{128,192},{192,0},{4,68},{68,132},{132,196},{196,4... | collective-permute-start | bytes 1179656 | tf_op jit(solution)/shard_map/ppermute | solution.py:199
  16.3 29.6 %collective-permute-start.7 = (f32[3,32,1024]{2,1,0:T(8,128)}, f32[3,32,1024]{2,1,0:T(8,128)S(1)}, u32[]{:S(2)}, u32[]{:S(2)}) collective-permute-start(f32[3,32,1024]{2,1,0:T(8,128)} %get-tuple-element.24), channel_id=1, source_target_pairs={{0,66},{64,130},{128,194},{192,2},{4,70},{68,134},{132,198},{196,6... | collective-permute-start | bytes 1179656 | tf_op jit(solution)/shard_map/ppermute | solution.py:199
  17.6 28.3 %collective-permute-start.8 = (f32[3,32,1024]{2,1,0:T(8,128)}, f32[3,32,1024]{2,1,0:T(8,128)S(1)}, u32[]{:S(2)}, u32[]{:S(2)}) collective-permute-start(f32[3,32,1024]{2,1,0:T(8,128)} %get-tuple-element.25), channel_id=1, source_target_pairs={{0,128},{64,192},{128,0},{192,64},{4,132},{68,196},{132,4},{196,68... | collective-permute-start | bytes 1179656 | tf_op jit(solution)/shard_map/ppermute | solution.py:199
  18.3 27.6 %collective-permute-start.9 = (f32[3,32,1024]{2,1,0:T(8,128)}, f32[3,32,1024]{2,1,0:T(8,128)S(1)}, u32[]{:S(2)}, u32[]{:S(2)}) collective-permute-start(f32[3,32,1024]{2,1,0:T(8,128)} %get-tuple-element.26), channel_id=1, source_target_pairs={{0,130},{64,194},{128,2},{192,66},{4,134},{68,198},{132,6},{196,70... | collective-permute-start | bytes 1179656 | tf_op jit(solution)/shard_map/ppermute | solution.py:199
  26.2 24.2 %copy-start.4 = (f32[3,32,1024]{2,1,0:T(8,128)}, f32[3,32,1024]{2,1,0:T(8,128)S(1)}, u32[]{:S(2)}) copy-start(f32[3,32,1024]{2,1,0:T(8,128)S(1)} %collective-permute-done.5.refs_1_) | copy-start | bytes 1179652
  26.2 19.7 %collective-permute-start.10 = (f32[3,32,1024]{2,1,0:T(8,128)}, f32[3,32,1024]{2,1,0:T(8,128)S(1)}, u32[]{:S(2)}, u32[]{:S(2)}) collective-permute-start(f32[3,32,1024]{2,1,0:T(8,128)} %get-tuple-element.27), channel_id=1, source_target_pairs={{0,192},{64,0},{128,64},{192,128},{4,196},{68,4},{132,68},{196,132... | collective-permute-start | bytes 1179656 | tf_op jit(solution)/shard_map/ppermute | solution.py:199
  26.9 23.5 %copy-start.5 = (f32[3,32,1024]{2,1,0:T(8,128)}, f32[3,32,1024]{2,1,0:T(8,128)S(1)}, u32[]{:S(2)}) copy-start(f32[3,32,1024]{2,1,0:T(8,128)S(1)} %collective-permute-done.6.refs_2_) | copy-start | bytes 1179652
  26.9 23.4 %collective-permute-start.11 = (f32[3,32,1024]{2,1,0:T(8,128)}, f32[3,32,1024]{2,1,0:T(8,128)S(1)}, u32[]{:S(2)}, u32[]{:S(2)}) collective-permute-start(f32[3,32,1024]{2,1,0:T(8,128)} %get-tuple-element.28), channel_id=1, source_target_pairs={{0,194},{64,2},{128,66},{192,130},{4,198},{68,6},{132,70},{196,134... | collective-permute-start | bytes 1179656 | tf_op jit(solution)/shard_map/ppermute | solution.py:199
  45.9 4.5 %copy-start.6 = (f32[3,32,1024]{2,1,0:T(8,128)}, f32[3,32,1024]{2,1,0:T(8,128)S(1)}, u32[]{:S(2)}) copy-start(f32[3,32,1024]{2,1,0:T(8,128)S(1)} %collective-permute-done.7.refs_3_) | copy-start | bytes 1179652
  45.9 4.5 %copy-start.7 = (f32[3,32,1024]{2,1,0:T(8,128)}, f32[3,32,1024]{2,1,0:T(8,128)S(1)}, u32[]{:S(2)}) copy-start(f32[3,32,1024]{2,1,0:T(8,128)S(1)} %collective-permute-done.8.refs_4_) | copy-start | bytes 1179652
  45.9 4.5 %copy-start.8 = (f32[3,32,1024]{2,1,0:T(8,128)}, f32[3,32,1024]{2,1,0:T(8,128)S(1)}, u32[]{:S(2)}) copy-start(f32[3,32,1024]{2,1,0:T(8,128)S(1)} %collective-permute-done.9.refs_5_) | copy-start | bytes 1179652
  45.9 4.5 %copy-start.9 = (f32[3,32,1024]{2,1,0:T(8,128)}, f32[3,32,1024]{2,1,0:T(8,128)S(1)}, u32[]{:S(2)}) copy-start(f32[3,32,1024]{2,1,0:T(8,128)S(1)} %collective-permute-done.10.refs_6_) | copy-start | bytes 1179652
  50.3 0.8 copy-start.10
  57.1 3.5 %copy-start.1 = (f32[3,32,1024]{2,1,0:T(8,128)S(1)}, f32[3,32,1024]{2,1,0:T(8,128)}, u32[]{:S(2)}) copy-start(f32[3,32,1024]{2,1,0:T(8,128)} %factor_slice.1) | copy-start | bytes 1179652
  57.1 3.1 %collective-permute-start.12 = (f32[3,32,1024]{2,1,0:T(8,128)}, f32[3,32,1024]{2,1,0:T(8,128)}, u32[]{:S(2)}, u32[]{:S(2)}) collective-permute-start(f32[3,32,1024]{2,1,0:T(8,128)} %factor_slice.1), channel_id=1, source_target_pairs={{0,1},{2,3},{64,65},{66,67},{128,129},{130,131},{192,193},{194,195... | collective-permute-start | bytes 1179656 | tf_op jit(solution)/shard_map/ppermute | solution.py:210
  60.7 0.7 copy-start.2
  61.4 18.1 %collective-permute-start.20 = (f32[3,16,1024]{2,1,0:T(8,128)S(1)}, f32[3,16,1024]{2,1,0:T(8,128)S(1)}, u32[]{:S(2)}, u32[]{:S(2)}) collective-permute-start(f32[3,16,1024]{2,1,0:T(8,128)S(1)} %constant_dynamic-slice_fusion), channel_id=1, source_target_pairs={{0,0},{1,4},{2,8},{3,12},{4,1},{5,5},{6,9},{7,13},{8,2},{9,6},{10,... | collective-permute-start | bytes 589832 | tf_op jit(solution)/shard_map/ppermute | solution.py:220
  79.6 0.7 copy-start.11
  80.3 8.2 %collective-permute-start.13 = (f32[3,32,1024]{2,1,0:T(8,128)}, f32[3,32,1024]{2,1,0:T(8,128)}, u32[]{:S(2)}, u32[]{:S(2)}) collective-permute-start(f32[3,32,1024]{2,1,0:T(8,128)} %copy-done.2), channel_id=1, source_target_pairs={{0,2},{2,64},{64,66},{66,128},{128,130},{130,192},{192,194},{194,0... | collective-permute-start | bytes 1179656 | tf_op jit(solution)/shard_map/ppermute | solution.py:230
  88.5 19.9 %collective-permute-start.15 = (f32[3,32,1024]{2,1,0:T(8,128)}, f32[3,32,1024]{2,1,0:T(8,128)S(1)}, u32[]{:S(2)}, u32[]{:S(2)}) collective-permute-start(f32[3,32,1024]{2,1,0:T(8,128)} %collective-permute-done.13), channel_id=1, source_target_pairs={{0,2},{2,64},{64,66},{66,128},{128,130},{130,192},{192,194},{194,0... | collective-permute-start | bytes 1179656 | tf_op jit(solution)/shard_map/ppermute | solution.py:230
  88.5 24.7 %collective-permute-start.14 = (f32[3,32,1024]{2,1,0:T(8,128)}, f32[3,32,1024]{2,1,0:T(8,128)}, u32[]{:S(2)}, u32[]{:S(2)}) collective-permute-start(f32[3,32,1024]{2,1,0:T(8,128)} %collective-permute-done.13), channel_id=1, source_target_pairs={{0,1},{1,0},{2,3},{3,2},{64,65},{65,64},{66,67},{67,66},{128,129},... | collective-permute-start | bytes 1179656 | tf_op jit(solution)/shard_map/ppermute | solution.py:233
  105.4 131.1 %collective-permute-start = (f32[512,512]{1,0:T(8,128)}, f32[512,512]{1,0:T(8,128)}, u32[]{:S(2)}, u32[]{:S(2)}) collective-permute-start(f32[512,512]{1,0:T(8,128)} %get-tuple-element.17), channel_id=1, source_target_pairs={{0,0},{1,64},{2,128},{3,192},{64,1},{65,65},{66,129},{67,193},{128... | collective-permute-start | bytes 3145736 | tf_op jit(solution)/shard_map/ppermute | solution.py:203
  107.3 129.2 %collective-permute-start.1 = (f32[512,512]{1,0:T(8,128)}, f32[512,512]{1,0:T(8,128)}, u32[]{:S(2)}, u32[]{:S(2)}) collective-permute-start(f32[512,512]{1,0:T(8,128)} %get-tuple-element.18), channel_id=1, source_target_pairs={{0,1},{1,65},{2,129},{3,193},{64,2},{65,66},{66,130},{67,194},{128... | collective-permute-start | bytes 3145736 | tf_op jit(solution)/shard_map/ppermute | solution.py:203
  108.3 56.5 %collective-permute-start.17 = (f32[3,32,1024]{2,1,0:T(8,128)S(1)}, f32[3,32,1024]{2,1,0:T(8,128)S(1)}, u32[]{:S(2)}, u32[]{:S(2)}) collective-permute-start(f32[3,32,1024]{2,1,0:T(8,128)S(1)} %collective-permute-done.15), channel_id=1, source_target_pairs={{0,2},{2,64},{64,66},{66,128},{128,130},{130,192},{192,194},{194,0... | collective-permute-start | bytes 1179656 | tf_op jit(solution)/shard_map/ppermute | solution.py:230
  112.1 52.7 %collective-permute-start.16 = (f32[3,32,1024]{2,1,0:T(8,128)S(1)}, f32[3,32,1024]{2,1,0:T(8,128)S(1)}, u32[]{:S(2)}, u32[]{:S(2)}) collective-permute-start(f32[3,32,1024]{2,1,0:T(8,128)S(1)} %collective-permute-done.15), channel_id=1, source_target_pairs={{0,1},{1,0},{2,3},{3,2},{64,65},{65,64},{66,67},{67,66},{128,129},... | collective-permute-start | bytes 1179656 | tf_op jit(solution)/shard_map/ppermute | solution.py:233
  113.2 123.4 %collective-permute-start.2 = (f32[512,512]{1,0:T(8,128)}, f32[512,512]{1,0:T(8,128)}, u32[]{:S(2)}, u32[]{:S(2)}) collective-permute-start(f32[512,512]{1,0:T(8,128)} %get-tuple-element.19), channel_id=1, source_target_pairs={{0,2},{1,66},{2,130},{3,194},{64,3},{65,67},{66,131},{67,195},{128... | collective-permute-start | bytes 3145736 | tf_op jit(solution)/shard_map/ppermute | solution.py:203
  164.8 71.8 %collective-permute-start.3 = (f32[512,512]{1,0:T(8,128)}, f32[512,512]{1,0:T(8,128)}, u32[]{:S(2)}, u32[]{:S(2)}) collective-permute-start(f32[512,512]{1,0:T(8,128)} %get-tuple-element.20), channel_id=1, source_target_pairs={{0,3},{1,67},{2,131},{3,195},{64,0},{65,64},{66,128},{67,192},{128... | collective-permute-start | bytes 3145736 | tf_op jit(solution)/shard_map/ppermute | solution.py:203
  164.8 31.9 %collective-permute-start.18 = (f32[3,32,1024]{2,1,0:T(8,128)S(1)}, f32[3,32,1024]{2,1,0:T(8,128)S(1)}, u32[]{:S(2)}, u32[]{:S(2)}) collective-permute-start(f32[3,32,1024]{2,1,0:T(8,128)S(1)} %collective-permute-done.17), channel_id=1, source_target_pairs={{0,1},{1,0},{2,3},{3,2},{64,65},{65,64},{66,67},{67,66},{128,129},... | collective-permute-start | bytes 1179656 | tf_op jit(solution)/shard_map/ppermute | solution.py:233
  196.7 39.8 %collective-permute-start.19 = (f32[3,32,1024]{2,1,0:T(8,128)S(1)}, f32[3,32,1024]{2,1,0:T(8,128)S(1)}, u32[]{:S(2)}, u32[]{:S(2)}) collective-permute-start(f32[3,32,1024]{2,1,0:T(8,128)S(1)} %collective-permute-done.17), channel_id=1, source_target_pairs={{0,2},{2,64},{64,66},{66,128},{128,130},{130,192},{192,194},{194,0... | collective-permute-start | bytes 1179656 | tf_op jit(solution)/shard_map/ppermute | solution.py:230
  236.5 1.7 copy-start
Sparse Core Ops, SparseCore 0:
  80.4 61.5 all-gather.2

commit v2 on v1

--- a/solution.py
+++ b/solution.py
@@ -128,59 +128,123 @@
     )(ids, *parts, pivot)
 
 
-def final_kernel(ids, cmap, front, r0, r1, r2, r3, left, right, out):
+def region(ids, p, q):
+    row_block = 3 * ids[1] + p
+    col_block = 3 * (4 * ids[0] + ids[2]) + q
+    return row_block >= 4, col_block
+
+
+def sender(ids, j):
+    return (ids[2] - j + 4) % 4
+
+
+def lands(ids, cmap, j, p, q):
+    child = sender(ids, j)
+    group = 4 * ids[0] + ids[2]
+    return (place(cmap, child, ids[1], p)[1] * place(cmap, child, group, q)[1]).astype(F32)
+
+
+def arrival(j):
+    def where(p, q, ids, cmap):
+        child = sender(ids, j)
+        return (
+            place(cmap, child, ids[1], p)[0],
+            place(cmap, child, 4 * ids[0] + ids[2], q)[0],
+        )
+
+    return pl.BlockSpec((BLK, BLK), where)
+
+
+TILE = pl.BlockSpec((BLK, BLK), lambda p, q, ids, cmap: (p, q))
+
+
+def update_kernel(ids, cmap, front, r0, r1, r2, *refs):
+    left, right, out = refs[:3]
+    left_hi, left_lo, right_hi, right_lo = refs[3:]
     p = pl.program_id(0)
     q = pl.program_id(1)
-    row = ids[1]
-    group = 4 * ids[0] + ids[2]
+
+    @pl.when(q == 0)
+    def _():
+        hi, lo = split(left[...].reshape(BLK, PANEL))
+        left_hi[...] = hi
+        left_lo[...] = lo
+
+    @pl.when(p == 0)
+    def _():
+        hi, lo = split(right[...].reshape(BLK, PANEL))
+        right_hi[q] = hi
+        right_lo[q] = lo
+
     value = front[...]
-    for j, ref in enumerate((r0, r1, r2, r3)):
-        child = (ids[2] - j + 4) % 4
-        ok = place(cmap, child, row, p)[1] * place(cmap, child, group, q)[1]
-        value = value + ref[...] * ok.astype(F32)
-    row_block = 3 * row + p
-    col_block = 3 * group + q
+    for j, ref in enumerate((r0, r1, r2)):
+        value = value + ref[...] * lands(ids, cmap, j, p, q)
+    below, col_block = region(ids, p, q)
     out[...] = value
 
-    @pl.when((row_block >= 4) & (col_block < 4))
+    @pl.when(below & (col_block < 4))
     def _():
         cols = pl.ds(pl.multiple_of(jnp.minimum(col_block, 3) * BLK, BLK), BLK)
         out[...] = left[:, 0, :, cols].reshape(BLK, BLK)
 
-    @pl.when((row_block >= 4) & (col_block >= 4))
-    def _():
-        out[...] = value - times_transposed(left[...].reshape(BLK, PANEL), right[...].reshape(BLK, PANEL))
-
-
-def final(ids, cmap, front, arrived, left, right):
-    def from_child(j):
-        def where(p, q, ids, cmap):
-            child = (ids[2] - j + 4) % 4
-            return (
-                place(cmap, child, ids[1], p)[0],
-                place(cmap, child, 4 * ids[0] + ids[2], q)[0],
-            )
-
-        return pl.BlockSpec((BLK, BLK), where)
-
-    tile = pl.BlockSpec((BLK, BLK), lambda p, q, ids, cmap: (p, q))
-    return pl.pallas_call(
-        final_kernel,
+    @pl.when(below & (col_block >= 4))
+    def _():
+        def dot(a, b):
+            return lax.dot_general(a, b, (((1,), (1,)), ((), ())), preferred_element_type=F32)
+
+        lh, ll, rh, rl = left_hi[...], left_lo[...], right_hi[q], right_lo[q]
+        out[...] = value - (dot(lh, rl) + dot(ll, rh) + dot(lh, rh))
+
+
+def update(ids, cmap, front, arrived, left, right):
+    return pl.pallas_call(
+        update_kernel,
         grid_spec=pltpu.PrefetchScalarGridSpec(
             num_scalar_prefetch=2,
             grid=(3, 3),
-            in_specs=[tile]
-            + [from_child(j) for j in range(4)]
+            in_specs=[TILE]
+            + [arrival(j) for j in range(3)]
+            + [pl.BlockSpec((16, 1, 16, PANEL), lambda p, q, ids, cmap: (0, p, 0, 0))]
             + [
-                pl.BlockSpec((8, 1, 32, PANEL), lambda p, q, ids, cmap: (0, p, 0, 0)),
-                pl.BlockSpec((16, 1, 16, PANEL), lambda p, q, ids, cmap: (0, q, 0, 0)),
+                pl.BlockSpec(
+                    (16, 1, 16, PANEL), lambda p, q, ids, cmap: (0, jnp.where(p == 0, q, 2), 0, 0)
+                )
             ],
-            out_specs=tile,
+            out_specs=TILE,
+            scratch_shapes=[
+                pltpu.VMEM((BLK, PANEL), jnp.bfloat16),
+                pltpu.VMEM((BLK, PANEL), jnp.bfloat16),
+                pltpu.VMEM((3, BLK, PANEL), jnp.bfloat16),
+                pltpu.VMEM((3, BLK, PANEL), jnp.bfloat16),
+            ],
         ),
         out_shape=jax.ShapeDtypeStruct((3 * BLK, 3 * BLK), F32),
         compiler_params=PARAMS,
-        name="final",
+        name="update",
     )(ids, cmap, front, *arrived, left, right)
+
+
+def finish_kernel(ids, cmap, partial, r3, out):
+    p = pl.program_id(0)
+    q = pl.program_id(1)
+    below, col_block = region(ids, p, q)
+    adds = jnp.where(below & (col_block < 4), 0.0, lands(ids, cmap, 3, p, q))
+    out[...] = partial[...] + r3[...] * adds
+
+
+def finish(ids, cmap, partial, last):
+    return pl.pallas_call(
+        finish_kernel,
+        grid_spec=pltpu.PrefetchScalarGridSpec(
+            num_scalar_prefetch=2,
+            grid=(3, 3),
+            in_specs=[TILE, arrival(3)],
+            out_specs=TILE,
+        ),
+        out_shape=jax.ShapeDtypeStruct((3 * BLK, 3 * BLK), F32),
+        compiler_params=PARAMS,
+        name="finish",
+    )(ids, cmap, partial, last)
 
 
 def shards(front_in, child_updates, pattern, child_map, pivot_inverse):
@@ -189,22 +253,21 @@
     col = lax.axis_index("col")
     ids = jnp.stack([sub, row, col]).astype(jnp.int32)
     core = col % 2
-    z = 2 * sub + col // 2
     pat = pattern[0]
 
+    def send(j):
+        return lax.ppermute(
+            sent[j], RING, [(4 * s + c, 4 * c + (s + j) % 4) for s in range(4) for c in range(4)]
+        )
+
     last = lax.ppermute(front_in[:, :BLK], RING, [(1, 0)])
+    sent = masked_groups(ids, pat, child_updates)
     slices = panel_slices(ids, pat, child_map, child_updates, front_in, last)
     parts = [slices[0]]
     for d in range(1, 8):
         parts.append(lax.ppermute(slices[d], RING, [(4 * s, 2 * ((2 * s + d) % 8)) for s in range(4)]))
-
-    sent = masked_groups(ids, pat, child_updates)
-    arrived = [
-        lax.ppermute(
-            sent[j], RING, [(4 * s + c, 4 * c + (s + j) % 4) for s in range(4) for c in range(4)]
-        )
-        for j in range(4)
-    ]
+    parts, sent = lax.optimization_barrier((parts, sent))
+    arrived = [send(j) for j in range(4)]
 
     mine = factor_slice(ids, parts, pivot_inverse)
     other = lax.ppermute(mine, RING, [(2 * k, 2 * k + 1) for k in range(8)])
@@ -217,22 +280,11 @@
         for r in range(16)
         for c in range(4)
     ]
-    right = lax.all_gather(lax.ppermute(half, MESH, turn), "row", axis=0)
-
-    onward = [(2 * k, 2 * ((k + 1) % 8)) for k in range(8)]
-    onward += [(2 * k + 1, 2 * ((k - 1) % 8) + 1) for k in range(8)]
-    swap = [(k, k ^ 1) for k in range(16)]
-    step = 1 - 2 * core
-    left = jnp.zeros((8,) + mine.shape, F32)
-    left = lax.dynamic_update_slice_in_dim(left, mine[None], z, 0)
-    piece = mine
-    for t in range(1, 5):
-        piece = lax.ppermute(piece, RING, onward)
-        left = lax.dynamic_update_slice_in_dim(left, piece[None], (z - t * step) % 8, 0)
-        if t < 4:
-            swapped = lax.ppermute(piece, RING, swap)
-            left = lax.dynamic_update_slice_in_dim(left, swapped[None], (z + t * step) % 8, 0)
-    return final(ids, child_map, front_in, arrived, left, right)
+    turned = lax.ppermute(half, MESH, turn)
+    right = lax.all_to_all(jnp.broadcast_to(turned, (16,) + turned.shape), "row", 0, 0)
+    left = lax.all_gather(half, RING, axis=0)
+    partial = update(ids, child_map, front_in, arrived[:3], left, right)
+    return finish(ids, child_map, partial, arrived[3])
 
 
 def solution(mesh):

time: 258 us -> 236 us (0.915)
  starting transfers between devices: 74.5 us -> 36 us
  waiting for transfers between devices: 133 us -> 140 us
  Pallas kernels: 26.6 us -> 32.7 us
    ppermute x12 -> x5, starting transfers between devices: 64.4 us -> 17.9 us  [the longest x4 13.7 us: send(): lax.ppermute(sent[j], RING, [(4 * s + c, 4 * c + (s + j) % 4) for s in ra...]
    ppermute x12 -> x5, waiting for transfers between devices: 103 us -> 114 us  [the longest x4 96.8 us: send(): lax.ppermute(sent[j], RING, [(4 * s + c, 4 * c + (s + j) % 4) for s in ra...]
    all_to_all x0 -> x1, starting transfers between devices: none -> 8.88 us  [shards(): lax.all_to_all(jnp.broadcast_to(turned, (16,) + turned.shape), 'row', 0, 0)]
    pallas_call x1 -> x2, Pallas kernels: 11.8 us -> 18 us  [the longest x1 10.6 us: update(): pl.pallas_call(update_kernel, grid_spec=pltpu.PrefetchScalarGridSpec(num_...]
    ppermute x7, waiting for transfers between devices: 28.7 us -> 24.3 us  [shards(): lax.ppermute(slices[d], RING, [(4 * s, 2 * ((2 * s + d) % 8)) for s in ra...]
    unnamed x24 -> x22, local copies, waits for them, and re-layouts: 4.64 us -> 5.29 us
  transfers between devices with their start and end apart: 22 -> 16, of which waited for: 10 -> 8; matrix products, arithmetic and copies ran while one was open for 1% -> 1% of each run, Pallas kernels for 2% -> 6%
where the time goes in v2:
time: 236 us; the launch traced here: 233 us
  waiting for transfers between devices  140 us (59%)
  starting transfers between devices  36 us (15%)
  Pallas kernels  32.7 us (14%)
  between operations  13.6 us (6%)
  local copies, waits for them, and re-layouts  8.55 us (4%)
    ppermute x4, waiting for transfers between devices, send(): lax.ppermute(sent[j], RING, [(4 * s + c, 4 * c + (s + j) % 4) for s in ra...  96.8 us
    ppermute x7, waiting for transfers between devices, shards(): lax.ppermute(slices[d], RING, [(4 * s, 2 * ((2 * s + d) % 8)) for s in ra...  24.3 us
    ppermute x1, waiting for transfers between devices, shards(): turned = lax.ppermute(half, MESH, turn)  17.4 us
    ppermute x4, starting transfers between devices, send(): lax.ppermute(sent[j], RING, [(4 * s + c, 4 * c + (s + j) % 4) for s in ra...  13.7 us
    pallas_call x1, Pallas kernels, update(): pl.pallas_call(update_kernel, grid_spec=pltpu.PrefetchScalarGridSpec(num_...  10.6 us
    all_to_all x1, starting transfers between devices, shards(): lax.all_to_all(jnp.broadcast_to(turned, (16,) + turned.shape), 'row', 0, 0)  8.88 us
    pallas_call x1, Pallas kernels, finish(): pl.pallas_call(finish_kernel, grid_spec=pltpu.PrefetchScalarGridSpec(num_...  7.39 us
    ppermute x7, starting transfers between devices, shards(): lax.ppermute(slices[d], RING, [(4 * s, 2 * ((2 * s + d) % 8)) for s in ra...  7.2 us
  transfers between devices with their start and end apart: 16, of which 8 were waited for; matrix products, arithmetic and copies ran while one was open for 1% of the time, Pallas kernels for 6%

profile of v2, /device:TPU:32, one launch (start us, length us, event | category | flops | bytes accessed | tf_op | source)
XLA Modules:
  0.0 233.2 jit_solution(17388312104734772210)
XLA Ops:
  6.5 0.0 all-gather.3.cloned.1.call-start
  6.5 1.2 slice.3
  7.7 0.7 collective-permute-start
  8.4 0.7 pad_add_fusion.ids
  9.1 0.0 collective-permute-done.last
  9.1 0.9 copy-done.3
  10.0 4.3 %panel_slices.1 = (f32[3,32,1024]{2,1,0:T(8,128)}, f32[3,32,1024]{2,1,0:T(8,128)}, f32[3,32,1024]{2,1,0:T(8,128)}, f32[3,32,1024]{2,1,0:T(8,128)}, f32[3,32,1024...) custom-call(s32[3]{0:T(128)} %pad_add_fusion.ids, s32[2,8]{1,0:T(2,128)} %bitcast.6, ...), custom_call_target="tpu_custom_call" | custom-call | tf_op jit(solution)/shard_map/panel_slices/pallas_call | solution.py:88
  14.3 1.3 collective-permute-start.1
  15.6 0.7 collective-permute-start.2
  16.3 1.3 collective-permute-start.3
  17.6 0.7 collective-permute-start.4
  18.3 1.3 collective-permute-start.5
  19.6 6.6 %collective-permute-done.1.refs_1_ = f32[3,32,1024]{2,1,0:T(8,128)S(1)} collective-permute-done((f32[3,32,1024]{2,1,0:T(8,128)}, f32[3,32,1024]{2,1,0:T(8,128)S(1)}, u32[]{:S(2)}, u32[]{:S(2)}) %collective-permute-start.1) | collective-permute-done | bytes 393248 | tf_op jit(solution)/shard_map/ppermute | solution.py:268
  26.2 0.7 collective-permute-start.6
  26.9 0.0 collective-permute-done.2.refs_2_
  26.9 1.3 collective-permute-start.7
  28.2 4.4 %masked_groups.1 = (f32[512,512]{1,0:T(8,128)}, f32[512,512]{1,0:T(8,128)}, f32[512,512]{1,0:T(8,128)}, f32[512,512]{1,0:T(8,128)}) custom-call(s32[3]{0:T(128)} %pad_add_fusion.ids, s32[2,8]{1,0:T(2,128)} %bitcast.7, f32[1,512,2048]{2,1,0:T(8,128)} %refs_3_.1, f32[1,512,2048]{2,1,0:T(8,128)} %refs_3_.1, f32[1,512,2048]{2,1,0:T(8,128)} %refs_3_.1, ...), custom_call_target="tpu_custom_call" | custom-call | tf_op jit(solution)/shard_map/masked_groups/pallas_call | solution.py:53
  32.6 0.0 copy-done.4
  32.6 0.0 copy-done.5
  32.6 13.2 %collective-permute-done.3.refs_3_ = f32[3,32,1024]{2,1,0:T(8,128)S(1)} collective-permute-done((f32[3,32,1024]{2,1,0:T(8,128)}, f32[3,32,1024]{2,1,0:T(8,128)S(1)}, u32[]{:S(2)}, u32[]{:S(2)}) %collective-permute-start.3) | collective-permute-done | bytes 393248 | tf_op jit(solution)/shard_map/ppermute | solution.py:268
  45.9 0.0 collective-permute-done.4.refs_4_
  45.9 0.0 collective-permute-done.5.refs_5_
  45.9 0.0 collective-permute-done.6.refs_6_
  45.9 4.4 %collective-permute-done.7.refs_7_ = f32[3,32,1024]{2,1,0:T(8,128)S(1)} collective-permute-done((f32[3,32,1024]{2,1,0:T(8,128)}, f32[3,32,1024]{2,1,0:T(8,128)S(1)}, u32[]{:S(2)}, u32[]{:S(2)}) %collective-permute-start.7) | collective-permute-done | bytes 393248 | tf_op jit(solution)/shard_map/ppermute | solution.py:268
  50.4 0.7 copy-done.10
  51.1 6.0 %factor_slice.1 = f32[3,32,1024]{2,1,0:T(8,128)} custom-call(s32[3]{0:T(128)} %pad_add_fusion.ids, f32[3,32,1024]{2,1,0:T(8,128)} %get-tuple-element.44.refs_0_, f32[3,32,1024]{2,1,0:T(8,128)} %copy-done.4, f32[3,32,1024]{2,1,0:T(8,128)} %copy-done.5, f32[3,32,1024]{2,1,0:T(8,128)} %copy-done.6, f32[3,32,1024]{2,1,0:T(8,128)} %copy-done.7, ...), custom_call_target="tpu_custom_call" | custom-call | tf_op jit(solution)/shard_map/factor_slice/pallas_call | solution.py:121
  57.1 1.3 collective-permute-start.11
  58.4 1.5 collective-permute-done.11
  59.9 1.6 dynamic-slice_select_fusion
  61.6 0.0 all-gather.3.cloned.1.call-update
  61.6 4.2 %collective-permute-start.12 = (f32[3,16,1024]{2,1,0:T(8,128)}, f32[3,16,1024]{2,1,0:T(8,128)S(1)}, u32[]{:S(2)}, u32[]{:S(2)}) collective-permute-start(f32[3,16,1024]{2,1,0:T(8,128)} %dynamic-slice_select_fusion), channel_id=1, source_target_pairs={{0,0},{1,4},{2,8},{3,12},{4,1},{5,5},{6,9},{7,13},{8,2},{9,6},{10,... | collective-permute-start | bytes 589832 | tf_op jit(solution)/shard_map/ppermute | solution.py:283
  65.8 17.4 %collective-permute-done.12 = f32[3,16,1024]{2,1,0:T(8,128)S(1)} collective-permute-done((f32[3,16,1024]{2,1,0:T(8,128)}, f32[3,16,1024]{2,1,0:T(8,128)S(1)}, u32[]{:S(2)}, u32[]{:S(2)}) %collective-permute-start.12) | collective-permute-done | bytes 196640 | tf_op jit(solution)/shard_map/ppermute | solution.py:283
  83.2 2.1 broadcast_in_dim.3
  85.2 8.9 %all-to-all-start = ((f32[16,3,16,1024]{3,2,1,0:T(8,128)}), f32[16,3,16,1024]{3,2,1,0:T(8,128)S(1)}, u32[]{:S(2)}, u32[]{:S(2)}) async-start(f32[16,3,16,1024]{3,2,1,0:T(8,128)} %broadcast_in_dim.3), calls=%async_computation | async-start | bytes 6291456 | tf_op jit(solution)/shard_map/all_to_all | solution.py:284
  94.1 6.6 %collective-permute-start.10 = (f32[512,512]{1,0:T(8,128)}, f32[512,512]{1,0:T(8,128)S(1)}, u32[]{:S(2)}, u32[]{:S(2)}) collective-permute-start(f32[512,512]{1,0:T(8,128)} %get-tuple-element.43), channel_id=1, source_target_pairs={{0,2},{1,66},{2,130},{3,194},{64,3},{65,67},{66,131},{67,195},{128... | collective-permute-start | bytes 3145736 | tf_op jit(solution)/shard_map/ppermute | solution.py:259
  100.7 7.0 %collective-permute-start.8 = (f32[512,512]{1,0:T(8,128)}, f32[512,512]{1,0:T(8,128)S(1)}, u32[]{:S(2)}, u32[]{:S(2)}) collective-permute-start(f32[512,512]{1,0:T(8,128)} %get-tuple-element.41), channel_id=1, source_target_pairs={{0,0},{1,64},{2,128},{3,192},{64,1},{65,65},{66,129},{67,193},{128... | collective-permute-start | bytes 3145736 | tf_op jit(solution)/shard_map/ppermute | solution.py:259
  107.7 0.1 collective-permute-start.9
  107.8 0.1 collective-permute-start.13
  107.9 36.8 %collective-permute-done.10.r2 = f32[512,512]{1,0:T(8,128)S(1)} collective-permute-done((f32[512,512]{1,0:T(8,128)}, f32[512,512]{1,0:T(8,128)S(1)}, u32[]{:S(2)}, u32[]{:S(2)}) %collective-permute-start.10) | collective-permute-done | bytes 1048608 | tf_op jit(solution)/shard_map/ppermute | solution.py:259
  144.7 0.0 collective-permute-done.8.r0
  144.7 1.0 copy-done.1
  145.7 1.0 copy-done.2
  146.6 36.6 %collective-permute-done.9.r1 = f32[512,512]{1,0:T(8,128)} collective-permute-done((f32[512,512]{1,0:T(8,128)}, f32[512,512]{1,0:T(8,128)}, u32[]{:S(2)}, u32[]{:S(2)}) %collective-permute-start.9) | collective-permute-done | bytes 1048608 | tf_op jit(solution)/shard_map/ppermute | solution.py:259
  183.3 0.0 all-to-all-done.refs_1_
  183.3 1.7 copy-done
  185.0 10.6 %update.1.partial = f32[768,768]{1,0:T(8,128)} custom-call(s32[3]{0:T(128)} %pad_add_fusion.ids, s32[4,32]{1,0:T(4,128)} %cmap.5, f32[768,768]{1,0:T(8,128)} %front.3, f32[512,512]{1,0:T(8,128)} %copy-done.2, f32[512,512]{1,0:T(8,128)} %collective-permute-done.9.r1, f32[512,512]{1,0:T(8,128)} %copy-done.1, f32[16,3,16,1024]{3,2,1,0:T(8,128)} %bitcast.5, ...), custom_call_target="tpu_custom_call" | custom-call | tf_op jit(solution)/shard_map/update/pallas_call | solution.py:200
  195.5 23.4 %collective-permute-done.13.r3 = f32[512,512]{1,0:T(8,128)} collective-permute-done((f32[512,512]{1,0:T(8,128)}, f32[512,512]{1,0:T(8,128)}, u32[]{:S(2)}, u32[]{:S(2)}) %collective-permute-start.13) | collective-permute-done | bytes 1048608 | tf_op jit(solution)/shard_map/ppermute | solution.py:259
  218.9 7.4 %finish.1 = f32[768,768]{1,0:T(8,128)} custom-call(s32[3]{0:T(128)} %pad_add_fusion.ids, s32[4,32]{1,0:T(4,128)} %cmap.5, f32[768,768]{1,0:T(8,128)} %update.1.partial, f32[512,512]{1,0:T(8,128)} %collective-permute-done.13.r3), custom_call_target="tpu_custom_call" | custom-call | tf_op jit(solution)/shard_map/finish/pallas_call | solution.py:236
  (16 shorter events, 0.0 us)
Async XLA Ops:
  6.5 176.7 %all-gather.3.cloned.1.call-start = ((), (), s32[]{:S(2)}) async-start(), calls=%async_computation.1 | async-start | bytes 3342336 | tf_op jit(solution)/shard_map/all_gather | solution.py:285
  7.7 1.4 collective-permute-start
  9.1 0.9 copy-start.3
  14.3 11.9 %collective-permute-start.1 = (f32[3,32,1024]{2,1,0:T(8,128)}, f32[3,32,1024]{2,1,0:T(8,128)S(1)}, u32[]{:S(2)}, u32[]{:S(2)}) collective-permute-start(f32[3,32,1024]{2,1,0:T(8,128)} %get-tuple-element.30), channel_id=1, source_target_pairs={{0,2},{64,66},{128,130},{192,194},{4,6},{68,70},{132,134},{196,198... | collective-permute-start | bytes 1179656 | tf_op jit(solution)/shard_map/ppermute | solution.py:268
  15.6 11.3 %collective-permute-start.2 = (f32[3,32,1024]{2,1,0:T(8,128)}, f32[3,32,1024]{2,1,0:T(8,128)S(1)}, u32[]{:S(2)}, u32[]{:S(2)}) collective-permute-start(f32[3,32,1024]{2,1,0:T(8,128)} %get-tuple-element.31), channel_id=1, source_target_pairs={{0,64},{64,128},{128,192},{192,0},{4,68},{68,132},{132,196},{196,4... | collective-permute-start | bytes 1179656 | tf_op jit(solution)/shard_map/ppermute | solution.py:268
  16.3 29.6 %collective-permute-start.3 = (f32[3,32,1024]{2,1,0:T(8,128)}, f32[3,32,1024]{2,1,0:T(8,128)S(1)}, u32[]{:S(2)}, u32[]{:S(2)}) collective-permute-start(f32[3,32,1024]{2,1,0:T(8,128)} %get-tuple-element.32), channel_id=1, source_target_pairs={{0,66},{64,130},{128,194},{192,2},{4,70},{68,134},{132,198},{196,6... | collective-permute-start | bytes 1179656 | tf_op jit(solution)/shard_map/ppermute | solution.py:268
  17.6 28.3 %collective-permute-start.4 = (f32[3,32,1024]{2,1,0:T(8,128)}, f32[3,32,1024]{2,1,0:T(8,128)S(1)}, u32[]{:S(2)}, u32[]{:S(2)}) collective-permute-start(f32[3,32,1024]{2,1,0:T(8,128)} %get-tuple-element.33), channel_id=1, source_target_pairs={{0,128},{64,192},{128,0},{192,64},{4,132},{68,196},{132,4},{196,68... | collective-permute-start | bytes 1179656 | tf_op jit(solution)/shard_map/ppermute | solution.py:268
  18.3 27.6 %collective-permute-start.5 = (f32[3,32,1024]{2,1,0:T(8,128)}, f32[3,32,1024]{2,1,0:T(8,128)S(1)}, u32[]{:S(2)}, u32[]{:S(2)}) collective-permute-start(f32[3,32,1024]{2,1,0:T(8,128)} %get-tuple-element.34), channel_id=1, source_target_pairs={{0,130},{64,194},{128,2},{192,66},{4,134},{68,198},{132,6},{196,70... | collective-permute-start | bytes 1179656 | tf_op jit(solution)/shard_map/ppermute | solution.py:268
  26.2 6.4 %copy-start.4 = (f32[3,32,1024]{2,1,0:T(8,128)}, f32[3,32,1024]{2,1,0:T(8,128)S(1)}, u32[]{:S(2)}) copy-start(f32[3,32,1024]{2,1,0:T(8,128)S(1)} %collective-permute-done.1.refs_1_) | copy-start | bytes 1179652
  26.2 19.7 %collective-permute-start.6 = (f32[3,32,1024]{2,1,0:T(8,128)}, f32[3,32,1024]{2,1,0:T(8,128)S(1)}, u32[]{:S(2)}, u32[]{:S(2)}) collective-permute-start(f32[3,32,1024]{2,1,0:T(8,128)} %get-tuple-element.35), channel_id=1, source_target_pairs={{0,192},{64,0},{128,64},{192,128},{4,196},{68,4},{132,68},{196,132... | collective-permute-start | bytes 1179656 | tf_op jit(solution)/shard_map/ppermute | solution.py:268
  26.9 5.7 %copy-start.5 = (f32[3,32,1024]{2,1,0:T(8,128)}, f32[3,32,1024]{2,1,0:T(8,128)S(1)}, u32[]{:S(2)}) copy-start(f32[3,32,1024]{2,1,0:T(8,128)S(1)} %collective-permute-done.2.refs_2_) | copy-start | bytes 1179652
  26.9 23.4 %collective-permute-start.7 = (f32[3,32,1024]{2,1,0:T(8,128)}, f32[3,32,1024]{2,1,0:T(8,128)S(1)}, u32[]{:S(2)}, u32[]{:S(2)}) collective-permute-start(f32[3,32,1024]{2,1,0:T(8,128)} %get-tuple-element.36), channel_id=1, source_target_pairs={{0,194},{64,2},{128,66},{192,130},{4,198},{68,6},{132,70},{196,134... | collective-permute-start | bytes 1179656 | tf_op jit(solution)/shard_map/ppermute | solution.py:268
  45.9 4.5 %copy-start.6 = (f32[3,32,1024]{2,1,0:T(8,128)}, f32[3,32,1024]{2,1,0:T(8,128)S(1)}, u32[]{:S(2)}) copy-start(f32[3,32,1024]{2,1,0:T(8,128)S(1)} %collective-permute-done.3.refs_3_) | copy-start | bytes 1179652
  45.9 4.5 %copy-start.7 = (f32[3,32,1024]{2,1,0:T(8,128)}, f32[3,32,1024]{2,1,0:T(8,128)S(1)}, u32[]{:S(2)}) copy-start(f32[3,32,1024]{2,1,0:T(8,128)S(1)} %collective-permute-done.4.refs_4_) | copy-start | bytes 1179652
  45.9 4.5 %copy-start.8 = (f32[3,32,1024]{2,1,0:T(8,128)}, f32[3,32,1024]{2,1,0:T(8,128)S(1)}, u32[]{:S(2)}) copy-start(f32[3,32,1024]{2,1,0:T(8,128)S(1)} %collective-permute-done.5.refs_5_) | copy-start | bytes 1179652
  45.9 4.5 %copy-start.9 = (f32[3,32,1024]{2,1,0:T(8,128)}, f32[3,32,1024]{2,1,0:T(8,128)S(1)}, u32[]{:S(2)}) copy-start(f32[3,32,1024]{2,1,0:T(8,128)S(1)} %collective-permute-done.6.refs_6_) | copy-start | bytes 1179652
  50.3 0.7 copy-start.10
  57.1 2.8 %collective-permute-start.11 = (f32[3,32,1024]{2,1,0:T(8,128)}, f32[3,32,1024]{2,1,0:T(8,128)S(1)}, u32[]{:S(2)}, u32[]{:S(2)}) collective-permute-start(f32[3,32,1024]{2,1,0:T(8,128)} %factor_slice.1), channel_id=1, source_target_pairs={{0,1},{2,3},{64,65},{66,67},{128,129},{130,131},{192,193},{194,195... | collective-permute-start | bytes 1179656 | tf_op jit(solution)/shard_map/ppermute | solution.py:273
  61.6 21.6 %collective-permute-start.12 = (f32[3,16,1024]{2,1,0:T(8,128)}, f32[3,16,1024]{2,1,0:T(8,128)S(1)}, u32[]{:S(2)}, u32[]{:S(2)}) collective-permute-start(f32[3,16,1024]{2,1,0:T(8,128)} %dynamic-slice_select_fusion), channel_id=1, source_target_pairs={{0,0},{1,4},{2,8},{3,12},{4,1},{5,5},{6,9},{7,13},{8,2},{9,6},{10,... | collective-permute-start | bytes 589832 | tf_op jit(solution)/shard_map/ppermute | solution.py:283
  85.2 98.0 %all-to-all-start = ((f32[16,3,16,1024]{3,2,1,0:T(8,128)}), f32[16,3,16,1024]{3,2,1,0:T(8,128)S(1)}, u32[]{:S(2)}, u32[]{:S(2)}) async-start(f32[16,3,16,1024]{3,2,1,0:T(8,128)} %broadcast_in_dim.3), calls=%async_computation | async-start | bytes 6291456 | tf_op jit(solution)/shard_map/all_to_all | solution.py:284
  94.1 50.5 %collective-permute-start.10 = (f32[512,512]{1,0:T(8,128)}, f32[512,512]{1,0:T(8,128)S(1)}, u32[]{:S(2)}, u32[]{:S(2)}) collective-permute-start(f32[512,512]{1,0:T(8,128)} %get-tuple-element.43), channel_id=1, source_target_pairs={{0,2},{1,66},{2,130},{3,194},{64,3},{65,67},{66,131},{67,195},{128... | collective-permute-start | bytes 3145736 | tf_op jit(solution)/shard_map/ppermute | solution.py:259
  100.7 44.0 %collective-permute-start.8 = (f32[512,512]{1,0:T(8,128)}, f32[512,512]{1,0:T(8,128)S(1)}, u32[]{:S(2)}, u32[]{:S(2)}) collective-permute-start(f32[512,512]{1,0:T(8,128)} %get-tuple-element.41), channel_id=1, source_target_pairs={{0,0},{1,64},{2,128},{3,192},{64,1},{65,65},{66,129},{67,193},{128... | collective-permute-start | bytes 3145736 | tf_op jit(solution)/shard_map/ppermute | solution.py:259
  107.7 75.6 %collective-permute-start.9 = (f32[512,512]{1,0:T(8,128)}, f32[512,512]{1,0:T(8,128)}, u32[]{:S(2)}, u32[]{:S(2)}) collective-permute-start(f32[512,512]{1,0:T(8,128)} %get-tuple-element.42), channel_id=1, source_target_pairs={{0,1},{1,65},{2,129},{3,193},{64,2},{65,66},{66,130},{67,194},{128... | collective-permute-start | bytes 3145736 | tf_op jit(solution)/shard_map/ppermute | solution.py:259
  107.8 111.1 %collective-permute-start.13 = (f32[512,512]{1,0:T(8,128)}, f32[512,512]{1,0:T(8,128)}, u32[]{:S(2)}, u32[]{:S(2)}) collective-permute-start(f32[512,512]{1,0:T(8,128)} %get-tuple-element.52), channel_id=1, source_target_pairs={{0,3},{1,67},{2,131},{3,195},{64,0},{65,64},{66,128},{67,192},{128... | collective-permute-start | bytes 3145736 | tf_op jit(solution)/shard_map/ppermute | solution.py:259
  144.6 1.0 copy-start.1
  145.7 1.0 copy-start.2
  183.3 1.7 copy-start
Sparse Core Ops, SparseCore 0:
  61.7 54.3 all-gather.2

commit v3 on v2

v3 whole, which is shorter than its diff:
```python
import jax
import jax.numpy as jnp
from jax import lax
from jax.experimental import pallas as pl
from jax.experimental.pallas import tpu as pltpu
from jax.sharding import PartitionSpec as P

BLK = 256
PANEL = 1024
RING = ("sub", "col")
MESH = ("sub", "row", "col")
SMEM = pl.BlockSpec(memory_space=pltpu.SMEM)
VMEM = pl.BlockSpec(memory_space=pltpu.VMEM)
PARAMS = pltpu.CompilerParams(vmem_limit_bytes=56 * 1024 * 1024)
F32 = jnp.float32


def split(x):
    hi = x.astype(jnp.bfloat16)
    return hi, (x - hi.astype(F32)).astype(jnp.bfloat16)


def place(cmap, child, group, slot):
    target = 3 * group + slot
    first = (cmap[child, 2 * group] == target).astype(jnp.int32)
    second = (cmap[child, 2 * group + 1] == target).astype(jnp.int32)
    return second, first + second


def mask_kernel(ids, pat, *refs):
    i = pl.program_id(0)
    for j in range(4):
        group = (ids[0] + j) % 4
        for b in range(2):
            cols = pl.ds(b * BLK, BLK)
            refs[4 + j][:, cols] = refs[j][0, :, cols] * pat[i, 2 * group + b].astype(F32)


def masked_groups(ids, pat, child):
    def group(j):
        return pl.BlockSpec((1, BLK, 2 * BLK), lambda i, ids, pat: (0, i, (ids[0] + j) % 4))

    return pl.pallas_call(
        mask_kernel,
        grid_spec=pltpu.PrefetchScalarGridSpec(
            num_scalar_prefetch=2,
            grid=(2,),
            in_specs=[group(j) for j in range(4)],
            out_specs=[pl.BlockSpec((BLK, 2 * BLK), lambda i, ids, pat: (i, 0))] * 4,
        ),
        out_shape=[jax.ShapeDtypeStruct((2 * BLK, 2 * BLK), F32)] * 4,
        compiler_params=PARAMS,
        name="masked_groups",
    )(ids, pat, child, child, child, child)


def panel_kernel(ids, pat, cmap, child, front, last, *outs):
    s = ids[0]
    row = ids[1]
    root = (s == 0).astype(F32)
    cols = [place(cmap, s, 0, q) for q in range(3)]
    cols.append((jnp.int32(2), (cmap[s, 2] == 3).astype(jnp.int32)))
    for p in range(3):
        a, a_ok = place(cmap, s, row, p)
        for q in range(4):
            b, b_ok = cols[q]
            weight = (pat[a, b] * a_ok * b_ok).astype(F32)
            for d in range(4):
                t = (s + d) % 4
                src = pl.multiple_of(a * BLK + t * 64, 64)
                own = pl.ds(pl.multiple_of(p * BLK + t * 64, 64), 64)
                value = child[0, pl.ds(src, 64), pl.ds(pl.multiple_of(b * BLK, BLK), BLK)] * weight
                kept = front[own, pl.ds(q * BLK, BLK)] if q < 3 else last[own, :]
                outs[d][p, :, pl.ds(q * BLK, BLK)] = value + kept * root


def panel_slices(ids, pat, cmap, child, front, last):
    return pl.pallas_call(
        panel_kernel,
        grid=(1,),
        in_specs=[
            SMEM,
            SMEM,
            SMEM,
            pl.BlockSpec((1, 2 * BLK, 3 * BLK), lambda i: (0, 0, 0)),
            pl.BlockSpec((3 * BLK, 3 * BLK), lambda i: (0, 0)),
            pl.BlockSpec((3 * BLK, BLK), lambda i: (0, 0)),
        ],
        out_specs=[pl.BlockSpec((3, 64, PANEL), lambda i: (0, 0, 0))] * 4,
        out_shape=[jax.ShapeDtypeStruct((3, 64, PANEL), F32)] * 4,
        compiler_params=PARAMS,
        name="panel_slices",
    )(ids, pat, cmap, child, front, last)


def pivot_kernel(pivot, hi, lo):
    hi[...], lo[...] = split(pivot[...])


def split_pivot(pivot):
    return pl.pallas_call(
        pivot_kernel,
        in_specs=[VMEM],
        out_specs=[VMEM, VMEM],
        out_shape=[jax.ShapeDtypeStruct((PANEL, PANEL), jnp.bfloat16)] * 2,
        compiler_params=PARAMS,
        name="split_pivot",
    )(pivot)


def dot(a, b):
    return lax.dot_general(a, b, (((1,), (1,)), ((), ())), preferred_element_type=F32)


def factor_kernel(*refs):
    parts, pivot_hi, pivot_lo, outs = refs[:4], refs[4], refs[5], refs[6:]
    value = parts[0][...]
    for ref in parts[1:]:
        value = value + ref[...]
    hi, lo = split(value.reshape(192, PANEL))
    ph, po = pivot_hi[...], pivot_lo[...]
    factor = (dot(hi, po) + dot(lo, ph) + dot(hi, ph)).reshape(3, 64, PANEL)
    for k in range(4):
        outs[k][...] = factor[:, 16 * k : 16 * k + 16]


def factor_slices(parts, pivot):
    return pl.pallas_call(
        factor_kernel,
        in_specs=[VMEM] * 6,
        out_specs=[VMEM] * 4,
        out_shape=[jax.ShapeDtypeStruct((3, 16, PANEL), F32)] * 4,
        compiler_params=PARAMS,
        name="factor_slices",
    )(*parts, *pivot)


def region(ids, p, q):
    row_block = 3 * ids[1] + p
    col_block = 3 * (4 * ids[0] + ids[2]) + q
    return row_block >= 4, col_block


def sender(ids, j):
    return (ids[2] - j + 4) % 4


def lands(ids, cmap, j, p, q):
    child = sender(ids, j)
    group = 4 * ids[0] + ids[2]
    return (place(cmap, child, ids[1], p)[1] * place(cmap, child, group, q)[1]).astype(F32)


def update_kernel(ids, assembled, *refs):
    left, right, out = refs[:3]
    left_hi, left_lo, right_hi, right_lo = refs[3:]
    p = pl.program_id(0)
    q = pl.program_id(1)

    @pl.when(q == 0)
    def _():
        hi, lo = split(left[...].reshape(BLK, PANEL))
        left_hi[...] = hi
        left_lo[...] = lo

    @pl.when(p == 0)
    def _():
        hi, lo = split(right[...].reshape(BLK, PANEL))
        right_hi[q] = hi
        right_lo[q] = lo

    value = assembled[...]
    below, col_block = region(ids, p, q)
    out[...] = value

    @pl.when(below & (col_block < 4))
    def _():
        cols = pl.ds(pl.multiple_of(jnp.minimum(col_block, 3) * BLK, BLK), BLK)
        out[...] = left[:, 0, :, cols].reshape(BLK, BLK)

    @pl.when(below & (col_block >= 4))
    def _():
        lh, ll, rh, rl = left_hi[...], left_lo[...], right_hi[q], right_lo[q]
        out[...] = value - (dot(lh, rl) + dot(ll, rh) + dot(lh, rh))


def update(ids, assembled, left, right):
    tile = pl.BlockSpec((BLK, BLK), lambda p, q, ids: (p, q))
    return pl.pallas_call(
        update_kernel,
        grid_spec=pltpu.PrefetchScalarGridSpec(
            num_scalar_prefetch=1,
            grid=(3, 3),
            in_specs=[tile]
            + [pl.BlockSpec((16, 1, 16, PANEL), lambda p, q, ids: (0, p, 0, 0))]
            + [
                pl.BlockSpec(
                    (16, 1, 16, PANEL), lambda p, q, ids: (0, jnp.where(p == 0, q, 2), 0, 0)
                )
            ],
            out_specs=tile,
            scratch_shapes=[
                pltpu.VMEM((BLK, PANEL), jnp.bfloat16),
                pltpu.VMEM((BLK, PANEL), jnp.bfloat16),
                pltpu.VMEM((3, BLK, PANEL), jnp.bfloat16),
                pltpu.VMEM((3, BLK, PANEL), jnp.bfloat16),
            ],
        ),
        out_shape=jax.ShapeDtypeStruct((3 * BLK, 3 * BLK), F32),
        compiler_params=PARAMS,
        name="update",
    )(ids, assembled, left, right)


def finish_kernel(ids, cmap, partial, r0, r1, r2, r3, r4, out):
    p = pl.program_id(0)
    group = 4 * ids[0] + ids[2]
    for q in range(3):
        cols = pl.ds(q * BLK, BLK)
        below, col_block = region(ids, p, q)
        kept = jnp.where(below & (col_block < 4), 0.0, 1.0)
        value = partial[:, cols]
        for j, ref in ((0, r0), (1, r1), (2, r2), (3, r3), (2, r4)):
            b = place(cmap, sender(ids, j), group, q)[0]
            src = pl.ds(pl.multiple_of(b * BLK, BLK), BLK)
            value = value + ref[:, src] * (lands(ids, cmap, j, p, q) * kept)
        out[:, cols] = value


def finish(ids, cmap, partial, arrived):
    def arrival(j):
        return pl.BlockSpec(
            (BLK, 2 * BLK), lambda p, ids, cmap: (place(cmap, sender(ids, j), ids[1], p)[0], 0)
        )

    band = pl.BlockSpec((BLK, 3 * BLK), lambda p, ids, cmap: (p, 0))
    return pl.pallas_call(
        finish_kernel,
        grid_spec=pltpu.PrefetchScalarGridSpec(
            num_scalar_prefetch=2,
            grid=(3,),
            in_specs=[band] + [arrival(j) for j in (0, 1, 2, 3, 2)],
            out_specs=band,
        ),
        out_shape=jax.ShapeDtypeStruct((3 * BLK, 3 * BLK), F32),
        compiler_params=PARAMS,
        name="finish",
    )(ids, cmap, partial, *arrived)


def shards(front_in, child_updates, pattern, child_map, pivot_inverse):
    sub = lax.axis_index("sub")
    row = lax.axis_index("row")
    col = lax.axis_index("col")
    ids = jnp.stack([sub, row, col]).astype(jnp.int32)
    pat = pattern[0]

    def at(s, r, c):
        return (s * 16 + r) * 4 + c

    def send(j):
        pairs = []
        for s in range(4):
            for r in range(16):
                for c in range(4):
                    group = 4 * c + (s + j) % 4
                    if (r < 2 or group > 0) and (s, group) not in ((3, 5), (0, 10)):
                        pairs.append((at(s, r, c), at(c, r, (s + j) % 4)))
        return lax.ppermute(sent[j], MESH, pairs)

    last = lax.ppermute(front_in[:, :BLK], RING, [(1, 0)])
    sent = masked_groups(ids, pat, child_updates)
    slices = panel_slices(ids, pat, child_map, child_updates, front_in, last)
    parts = [slices[0]]
    for d in range(1, 4):
        parts.append(lax.ppermute(slices[d], RING, [(4 * s, 4 * ((s + d) % 4)) for s in range(4)]))
    pieces = factor_slices(parts, split_pivot(pivot_inverse))
    mine = pieces[0]
    others = [lax.ppermute(pieces[k], RING, [(4 * s, 4 * s + k) for s in range(4)]) for k in range(1, 4)]
    mine = jnp.where(col == 0, mine, others[0] + others[1] + others[2])

    leg = lax.ppermute(
        sent[2],
        MESH,
        [(at(3, r, 1), at(2, r, 2)) for r in range(16)] + [(at(0, r, 2), at(1, r, 1)) for r in range(16)],
    )
    mine, leg = lax.optimization_barrier((mine, leg))

    turn = [
        (at(s, r, c), at(r // 4, 4 * s + c, r % 4)) for s in range(4) for r in range(16) for c in range(4)
    ]
    turned = lax.ppermute(mine, MESH, turn)
    turned, sent, leg = lax.optimization_barrier((turned, sent, leg))
    relayed = lax.ppermute(
        leg, MESH, [(at(s, r, s), at(3 - s, r, 3 - s)) for s in (1, 2) for r in range(16)]
    )

    def spread(turned):
        return lax.all_to_all(jnp.broadcast_to(turned, (16,) + turned.shape), "row", 0, 0)

    right = lax.cond(
        child_map[0, 0] >= 0, spread, lambda turned: jnp.zeros((16,) + turned.shape, F32), turned
    )
    left = lax.all_gather(mine, RING, axis=0)
    partial = update(ids, front_in, left, right)
    return finish(ids, child_map, partial, [send(j) for j in range(4)] + [relayed])


def solution(mesh):
    in_specs = (P("row", ("sub", "col")), P("sub", "row", "col"), P("sub", "row", "col"), P(), P())
    out_specs = P("row", ("sub", "col"))
    return jax.shard_map(shards, mesh=mesh, in_specs=in_specs, out_specs=out_specs, check_vma=False)
```

time: 236 us -> 229 us (0.970)
  the two profiles are of different devices: /device:TPU:32 before, /device:TPU:31 now
where the time goes in v3:
time: 229 us; the launch traced here: 228 us
  waiting for transfers between devices  74.3 us (32%)
  starting transfers between devices  48.5 us (21%)
  blocking collectives  48.3 us (21%)
  Pallas kernels  36.5 us (16%)
  between operations  14.1 us (6%)
  local copies, waits for them, and re-layouts  5.04 us (2%)
    all_to_all x1, blocking collectives, spread(): lax.all_to_all(jnp.broadcast_to(turned, (16,) + turned.shape), 'row', 0, 0)  48.3 us
    ppermute x1, starting transfers between devices, shards(): turned = lax.ppermute(mine, MESH, turn)  30.2 us
    ppermute x4, waiting for transfers between devices, send(): return lax.ppermute(sent[j], MESH, pairs)  27 us
    ppermute x1, waiting for transfers between devices, shards(): turned = lax.ppermute(mine, MESH, turn)  19.4 us
    ppermute x3, waiting for transfers between devices, shards(): lax.ppermute(pieces[k], RING, [(4 * s, 4 * s + k) for s in range(4)])  13.3 us
    all_gather x1, waiting for transfers between devices, shards(): left = lax.all_gather(mine, RING, axis=0)  13.3 us
    pallas_call x1, Pallas kernels, update(): pl.pallas_call(update_kernel, grid_spec=pltpu.PrefetchScalarGridSpec(num_...  10.1 us
    ppermute x4, starting transfers between devices, send(): return lax.ppermute(sent[j], MESH, pairs)  7.66 us
  transfers between devices with their start and end apart: 15, of which 7 were waited for; matrix products, arithmetic and copies ran while one was open for 1% of the time, Pallas kernels for 11%

profile of v3, /device:TPU:31, one launch (start us, length us, event | category | flops | bytes accessed | tf_op | source)
XLA Modules:
  0.0 228.0 jit_solution(5735246217080544100)
XLA Ops:
  6.5 0.0 all-gather.3.cloned.1.call-start
  6.5 1.2 slice.6
  7.7 2.6 %collective-permute-start = (f32[768,256]{1,0:T(8,128)S(1)}, f32[768,256]{1,0:T(8,128)S(1)}, u32[]{:S(2)}, u32[]{:S(2)}) collective-permute-start(f32[768,256]{1,0:T(8,128)S(1)} %slice.6), channel_id=1, source_target_pairs={{1,0},{5,4},{9,8},{13,12},{17,16},{21,20},{25,24},{29,28},{33,32},... | collective-permute-start | bytes 2359304 | tf_op jit(solution)/shard_map/ppermute | solution.py:271
  10.4 0.6 pad_add_fusion.ids
  10.9 1.3 collective-permute-done.last
  12.2 0.9 copy-done.3
  13.1 4.3 %panel_slices.1 = (f32[3,64,1024]{2,1,0:T(8,128)}, f32[3,64,1024]{2,1,0:T(8,128)}, f32[3,64,1024]{2,1,0:T(8,128)}, f32[3,64,1024]{2,1,0:T(8,128)}) custom-call(s32[3]{0:T(128)} %pad_add_fusion.ids, s32[2,8]{1,0:T(2,128)} %bitcast.7, s32[4,32]{1,0:T(4,128)} %cmap.3, f32[1,512,2048]{2,1,0:T(8,128)} %refs_3_.1, f32[768,768]{1,0:T(8,128)} %assembled.1, ...), custom_call_target="tpu_custom_call" | custom-call | tf_op jit(solution)/shard_map/panel_slices/pallas_call | solution.py:78
  17.4 0.7 collective-permute-start.1
  18.1 0.7 collective-permute-start.2
  18.9 0.7 collective-permute-start.3
  19.6 4.4 %masked_groups.1 = (f32[512,512]{1,0:T(8,128)}, f32[512,512]{1,0:T(8,128)}, f32[512,512]{1,0:T(8,128)}, f32[512,512]{1,0:T(8,128)}) custom-call(s32[3]{0:T(128)} %pad_add_fusion.ids, s32[2,8]{1,0:T(2,128)} %bitcast.8, f32[1,512,2048]{2,1,0:T(8,128)} %refs_3_.1, f32[1,512,2048]{2,1,0:T(8,128)} %refs_3_.1, f32[1,512,2048]{2,1,0:T(8,128)} %refs_3_.1, ...), custom_call_target="tpu_custom_call" | custom-call | tf_op jit(solution)/shard_map/masked_groups/pallas_call | solution.py:43
  24.0 1.6 collective-permute-start.7
  25.7 4.6 %split_pivot.1 = (bf16[1024,1024]{1,0:T(8,128)(2,1)}, bf16[1024,1024]{1,0:T(8,128)(2,1)}) custom-call(f32[1024,1024]{1,0:T(8,128)} %pivot.1), custom_call_target="tpu_custom_call" | custom-call | tf_op jit(solution)/shard_map/split_pivot/pallas_call | solution.py:101
  30.3 0.0 collective-permute-done.1.refs_1_
  30.3 0.0 collective-permute-done.2.refs_2_
  30.3 0.0 collective-permute-done.3.refs_3_
  30.3 0.9 copy-done
  31.2 0.3 copy-done.1
  31.4 0.3 copy-done.2
  31.7 6.3 %factor_slices.1 = (f32[3,16,1024]{2,1,0:T(8,128)}, f32[3,16,1024]{2,1,0:T(8,128)}, f32[3,16,1024]{2,1,0:T(8,128)}, f32[3,16,1024]{2,1,0:T(8,128)}) custom-call(f32[3,64,1024]{2,1,0:T(8,128)} %get-tuple-element.31.refs_0_, f32[3,64,1024]{2,1,0:T(8,128)} %copy-done, f32[3,64,1024]{2,1,0:T(8,128)} %copy-done.1, f32[3,64,1024]{2,1,0:T(8,128)} %copy-done.2, ...), custom_call_target="tpu_custom_call" | custom-call | tf_op jit(solution)/shard_map/factor_slices/pallas_call | solution.py:128
  38.0 1.3 collective-permute-start.4
  39.3 0.7 collective-permute-start.5
  40.0 0.7 collective-permute-start.6
  40.7 13.3 %collective-permute-done.4 = f32[3,16,1024]{2,1,0:T(8,128)S(1)} collective-permute-done((f32[3,16,1024]{2,1,0:T(8,128)}, f32[3,16,1024]{2,1,0:T(8,128)S(1)}, u32[]{:S(2)}, u32[]{:S(2)}) %collective-permute-start.4) | collective-permute-done | bytes 196640 | tf_op jit(solution)/shard_map/ppermute | solution.py:279
  54.0 0.0 collective-permute-done.5
  54.0 0.0 collective-permute-done.6
  54.0 0.7 add_select_fusion
  54.7 0.0 collective-permute-done.7
  54.7 0.0 all-gather.3.cloned.1.call-update
  54.7 30.2 %collective-permute-start.8 = (f32[3,16,1024]{2,1,0:T(8,128)}, f32[3,16,1024]{2,1,0:T(8,128)S(1)}, u32[]{:S(2)}, u32[]{:S(2)}) collective-permute-start(f32[3,16,1024]{2,1,0:T(8,128)} %add_select_fusion), channel_id=1, source_target_pairs={{0,0},{1,4},{2,8},{3,12},{4,1},{5,5},{6,9},{7,13},{8,2},{9,6},{10,... | collective-permute-start | bytes 589832 | tf_op jit(solution)/shard_map/ppermute | solution.py:292
  84.9 19.4 %collective-permute-done.8 = f32[3,16,1024]{2,1,0:T(8,128)S(1)} collective-permute-done((f32[3,16,1024]{2,1,0:T(8,128)}, f32[3,16,1024]{2,1,0:T(8,128)S(1)}, u32[]{:S(2)}, u32[]{:S(2)}) %collective-permute-start.8) | collective-permute-done | bytes 196640 | tf_op jit(solution)/shard_map/ppermute | solution.py:292
  104.3 1.9 collective-permute-start.10
  106.2 1.9 collective-permute-start.11
  108.2 1.9 collective-permute-start.12
  110.1 1.7 collective-permute-start.13
  111.7 1.9 collective-permute-start.9
  113.7 1.2 slice.7
  115.4 48.7 %conditional.1 = (f32[16,3,16,1024]{3,2,1,0:T(8,128)S(1)}) conditional(s32[]{:T(128)} %bitcast.5, () %tuple.14, f32[3,16,1024]{2,1,0:T(8,128)S(1)} %collective-permute-done.8), branch_computations={%region_0.1_spmd, %region_1.2_spmd} | conditional | bytes 9633800 | solution.py:301
  115.4 0.4 broadcast_in_dim.2
  115.8 48.3 %all_to_all.4 = f32[16,3,16,1024]{3,2,1,0:T(8,128)S(1)} all-to-all(f32[16,3,16,1024]{3,2,1,0:T(8,128)S(1)} %broadcast_in_dim.2), channel_id=1, replica_groups=mesh['sub'=4,'row'=16,'col'=4] {'row'}, dimensions={0} | all-to-all | bytes 6291456 | tf_op jit(solution)/shard_map/cond/branch_1_fun/all_to_all | solution.py:299
  164.1 13.3 %all-gather.3.cloned.1.call-done = f32[48,16,1024]{2,1,0:T(8,128)} async-done(((f32[3,16,1024]{2,1,0:T(8,128)}), f32[48,16,1024]{2,1,0:T(8,128)}) %all-gather.3.cloned.1.call-update) | async-done | bytes 3145744 | tf_op jit(solution)/shard_map/all_gather | solution.py:304
  177.4 10.1 %update.1.partial = f32[768,768]{1,0:T(8,128)} custom-call(s32[3]{0:T(128)} %pad_add_fusion.ids, f32[768,768]{1,0:T(8,128)} %assembled.1, f32[16,3,16,1024]{3,2,1,0:T(8,128)} %bitcast.6, f32[16,3,16,1024]{3,2,1,0:T(8,128)S(1)} %get-tuple-element.53.refs_1_), custom_call_target="tpu_custom_call" | custom-call | tf_op jit(solution)/shard_map/update/pallas_call | solution.py:189
  187.5 0.0 collective-permute-done.10.r1
  187.5 2.7 %collective-permute-done.11.r2 = f32[512,512]{1,0:T(8,128)} collective-permute-done((f32[512,512]{1,0:T(8,128)}, f32[512,512]{1,0:T(8,128)}, u32[]{:S(2)}, u32[]{:S(2)}) %collective-permute-start.11) | collective-permute-done | bytes 1048608 | tf_op jit(solution)/shard_map/ppermute | solution.py:269
  190.2 13.0 %collective-permute-done.12.r3 = f32[512,512]{1,0:T(8,128)} collective-permute-done((f32[512,512]{1,0:T(8,128)}, f32[512,512]{1,0:T(8,128)}, u32[]{:S(2)}, u32[]{:S(2)}) %collective-permute-start.12) | collective-permute-done | bytes 1048608 | tf_op jit(solution)/shard_map/ppermute | solution.py:269
  203.3 0.0 collective-permute-done.13.r4
  203.3 11.2 %collective-permute-done.9.r0 = f32[512,512]{1,0:T(8,128)} collective-permute-done((f32[512,512]{1,0:T(8,128)}, f32[512,512]{1,0:T(8,128)}, u32[]{:S(2)}, u32[]{:S(2)}) %collective-permute-start.9) | collective-permute-done | bytes 1048608 | tf_op jit(solution)/shard_map/ppermute | solution.py:269
  214.5 6.7 %finish.1 = f32[768,768]{1,0:T(8,128)} custom-call(s32[3]{0:T(128)} %pad_add_fusion.ids, s32[4,32]{1,0:T(4,128)} %cmap.3, f32[768,768]{1,0:T(8,128)} %update.1.partial, f32[512,512]{1,0:T(8,128)} %collective-permute-done.9.r0, f32[512,512]{1,0:T(8,128)} %collective-permute-done.10.r1, f32[512,512]{1,0:T(8,128)} %collective-permute-done.11.r2, ...), custom_call_target="tpu_custom_call" | custom-call | tf_op jit(solution)/shard_map/finish/pallas_call | solution.py:237
  (4 shorter events, 0.0 us)
Async XLA Ops:
  6.5 170.9 %all-gather.3.cloned.1.call-start = ((), (), s32[]{:S(2)}) async-start(), calls=%async_computation.1 | async-start | bytes 3342336 | tf_op jit(solution)/shard_map/all_gather | solution.py:304
  7.7 4.5 %collective-permute-start = (f32[768,256]{1,0:T(8,128)S(1)}, f32[768,256]{1,0:T(8,128)S(1)}, u32[]{:S(2)}, u32[]{:S(2)}) collective-permute-start(f32[768,256]{1,0:T(8,128)S(1)} %slice.6), channel_id=1, source_target_pairs={{1,0},{5,4},{9,8},{13,12},{17,16},{21,20},{25,24},{29,28},{33,32},... | collective-permute-start | bytes 2359304 | tf_op jit(solution)/shard_map/ppermute | solution.py:271
  12.2 0.9 copy-start.3
  17.4 12.8 %collective-permute-start.1 = (f32[3,64,1024]{2,1,0:T(8,128)}, f32[3,64,1024]{2,1,0:T(8,128)S(1)}, u32[]{:S(2)}, u32[]{:S(2)}) collective-permute-start(f32[3,64,1024]{2,1,0:T(8,128)} %get-tuple-element.32), channel_id=1, source_target_pairs={{0,64},{64,128},{128,192},{192,0},{4,68},{68,132},{132,196},{196,4... | collective-permute-start | bytes 2359304 | tf_op jit(solution)/shard_map/ppermute | solution.py:276
  18.1 12.1 %collective-permute-start.2 = (f32[3,64,1024]{2,1,0:T(8,128)}, f32[3,64,1024]{2,1,0:T(8,128)S(1)}, u32[]{:S(2)}, u32[]{:S(2)}) collective-permute-start(f32[3,64,1024]{2,1,0:T(8,128)} %get-tuple-element.33), channel_id=1, source_target_pairs={{0,128},{64,192},{128,0},{192,64},{4,132},{68,196},{132,4},{196,68... | collective-permute-start | bytes 2359304 | tf_op jit(solution)/shard_map/ppermute | solution.py:276
  18.9 11.4 %collective-permute-start.3 = (f32[3,64,1024]{2,1,0:T(8,128)}, f32[3,64,1024]{2,1,0:T(8,128)S(1)}, u32[]{:S(2)}, u32[]{:S(2)}) collective-permute-start(f32[3,64,1024]{2,1,0:T(8,128)} %get-tuple-element.34), channel_id=1, source_target_pairs={{0,192},{64,0},{128,64},{192,128},{4,196},{68,4},{132,68},{196,132... | collective-permute-start | bytes 2359304 | tf_op jit(solution)/shard_map/ppermute | solution.py:276
  24.0 30.7 %collective-permute-start.7 = (f32[512,512]{1,0:T(8,128)}, f32[512,512]{1,0:T(8,128)}, u32[]{:S(2)}, u32[]{:S(2)}) collective-permute-start(f32[512,512]{1,0:T(8,128)} %get-tuple-element.50), channel_id=1, source_target_pairs={{193,130},{197,134},{201,138},{205,142},{209,146},{213,150},{217,1... | collective-permute-start | bytes 3145736 | tf_op jit(solution)/shard_map/ppermute | solution.py:282
  30.3 0.9 copy-start
  30.3 1.2 copy-start.1
  30.3 1.4 copy-start.2
  38.0 16.0 %collective-permute-start.4 = (f32[3,16,1024]{2,1,0:T(8,128)}, f32[3,16,1024]{2,1,0:T(8,128)S(1)}, u32[]{:S(2)}, u32[]{:S(2)}) collective-permute-start(f32[3,16,1024]{2,1,0:T(8,128)} %get-tuple-element.38), channel_id=1, source_target_pairs={{0,1},{64,65},{128,129},{192,193},{4,5},{68,69},{132,133},{196,197... | collective-permute-start | bytes 589832 | tf_op jit(solution)/shard_map/ppermute | solution.py:279
  39.3 14.7 %collective-permute-start.5 = (f32[3,16,1024]{2,1,0:T(8,128)}, f32[3,16,1024]{2,1,0:T(8,128)S(1)}, u32[]{:S(2)}, u32[]{:S(2)}) collective-permute-start(f32[3,16,1024]{2,1,0:T(8,128)} %get-tuple-element.39), channel_id=1, source_target_pairs={{0,2},{64,66},{128,130},{192,194},{4,6},{68,70},{132,134},{196,198... | collective-permute-start | bytes 589832 | tf_op jit(solution)/shard_map/ppermute | solution.py:279
  40.0 14.0 %collective-permute-start.6 = (f32[3,16,1024]{2,1,0:T(8,128)}, f32[3,16,1024]{2,1,0:T(8,128)S(1)}, u32[]{:S(2)}, u32[]{:S(2)}) collective-permute-start(f32[3,16,1024]{2,1,0:T(8,128)} %get-tuple-element.40), channel_id=1, source_target_pairs={{0,3},{64,67},{128,131},{192,195},{4,7},{68,71},{132,135},{196,199... | collective-permute-start | bytes 589832 | tf_op jit(solution)/shard_map/ppermute | solution.py:279
  54.7 49.6 %collective-permute-start.8 = (f32[3,16,1024]{2,1,0:T(8,128)}, f32[3,16,1024]{2,1,0:T(8,128)S(1)}, u32[]{:S(2)}, u32[]{:S(2)}) collective-permute-start(f32[3,16,1024]{2,1,0:T(8,128)} %add_select_fusion), channel_id=1, source_target_pairs={{0,0},{1,4},{2,8},{3,12},{4,1},{5,5},{6,9},{7,13},{8,2},{9,6},{10,... | collective-permute-start | bytes 589832 | tf_op jit(solution)/shard_map/ppermute | solution.py:292
  104.3 83.2 %collective-permute-start.10 = (f32[512,512]{1,0:T(8,128)}, f32[512,512]{1,0:T(8,128)}, u32[]{:S(2)}, u32[]{:S(2)}) collective-permute-start(f32[512,512]{1,0:T(8,128)} %get-tuple-element.49), channel_id=1, source_target_pairs={{0,1},{1,65},{2,129},{3,193},{4,5},{5,69},{6,133},{7,197},{8,9},{9... | collective-permute-start | bytes 3145736 | tf_op jit(solution)/shard_map/ppermute | solution.py:269
  106.2 84.0 %collective-permute-start.11 = (f32[512,512]{1,0:T(8,128)}, f32[512,512]{1,0:T(8,128)}, u32[]{:S(2)}, u32[]{:S(2)}) collective-permute-start(f32[512,512]{1,0:T(8,128)} %get-tuple-element.50), channel_id=1, source_target_pairs={{0,2},{1,66},{3,194},{4,6},{5,70},{7,198},{8,10},{9,74},{11,202},{... | collective-permute-start | bytes 3145736 | tf_op jit(solution)/shard_map/ppermute | solution.py:269
  108.2 95.1 %collective-permute-start.12 = (f32[512,512]{1,0:T(8,128)}, f32[512,512]{1,0:T(8,128)}, u32[]{:S(2)}, u32[]{:S(2)}) collective-permute-start(f32[512,512]{1,0:T(8,128)} %get-tuple-element.51), channel_id=1, source_target_pairs={{0,3},{1,67},{2,131},{3,195},{4,7},{5,71},{6,135},{7,199},{8,11},{... | collective-permute-start | bytes 3145736 | tf_op jit(solution)/shard_map/ppermute | solution.py:269
  110.1 93.2 %collective-permute-start.13 = (f32[512,512]{1,0:T(8,128)}, f32[512,512]{1,0:T(8,128)}, u32[]{:S(2)}, u32[]{:S(2)}) collective-permute-start(f32[512,512]{1,0:T(8,128)} %collective-permute-done.7), channel_id=1, source_target_pairs={{65,130},{69,134},{73,138},{77,142},{81,146},{85,150},{89,154},{93... | collective-permute-start | bytes 3145736 | tf_op jit(solution)/shard_map/ppermute | solution.py:294
  111.7 102.8 %collective-permute-start.9 = (f32[512,512]{1,0:T(8,128)}, f32[512,512]{1,0:T(8,128)}, u32[]{:S(2)}, u32[]{:S(2)}) collective-permute-start(f32[512,512]{1,0:T(8,128)} %get-tuple-element.48), channel_id=1, source_target_pairs={{0,0},{1,64},{2,128},{3,192},{4,4},{5,68},{6,132},{7,196},{9,72},{... | collective-permute-start | bytes 3145736 | tf_op jit(solution)/shard_map/ppermute | solution.py:269
Sparse Core Ops, SparseCore 0:
  54.9 122.5 all-gather.2

commit v4 on v3

--- a/solution.py
+++ b/solution.py
@@ -94,7 +94,7 @@
 
 
 def pivot_kernel(pivot, hi, lo):
-    hi[...], lo[...] = split(pivot[...])
+    hi[...], lo[...] = split(pivot[...].T)
 
 
 def split_pivot(pivot):
@@ -110,6 +110,10 @@
 
 def dot(a, b):
     return lax.dot_general(a, b, (((1,), (1,)), ((), ())), preferred_element_type=F32)
+
+
+def times(a, b):
+    return lax.dot_general(a, b, (((1,), (0,)), ((), ())), preferred_element_type=F32)
 
 
 def factor_kernel(*refs):
@@ -119,7 +123,7 @@
         value = value + ref[...]
     hi, lo = split(value.reshape(192, PANEL))
     ph, po = pivot_hi[...], pivot_lo[...]
-    factor = (dot(hi, po) + dot(lo, ph) + dot(hi, ph)).reshape(3, 64, PANEL)
+    factor = (times(hi, po) + times(lo, ph) + times(hi, ph)).reshape(3, 64, PANEL)
     for k in range(4):
         outs[k][...] = factor[:, 16 * k : 16 * k + 16]
 
@@ -142,6 +146,8 @@
 
 
 def sender(ids, j):
+    if j == 5:
+        return jnp.where(ids[0] == 1, 2, jnp.where(ids[0] == 2, 1, ids[0]))
     return (ids[2] - j + 4) % 4
 
 
@@ -151,7 +157,7 @@
     return (place(cmap, child, ids[1], p)[1] * place(cmap, child, group, q)[1]).astype(F32)
 
 
-def update_kernel(ids, assembled, *refs):
+def update_kernel(ids, cmap, front, early, *refs):
     left, right, out = refs[:3]
     left_hi, left_lo, right_hi, right_lo = refs[3:]
     p = pl.program_id(0)
@@ -169,7 +175,7 @@
         right_hi[q] = hi
         right_lo[q] = lo
 
-    value = assembled[...]
+    value = front[...] + early[...] * lands(ids, cmap, 5, p, q)
     below, col_block = region(ids, p, q)
     out[...] = value
 
@@ -184,18 +190,25 @@
         out[...] = value - (dot(lh, rl) + dot(ll, rh) + dot(lh, rh))
 
 
-def update(ids, assembled, left, right):
-    tile = pl.BlockSpec((BLK, BLK), lambda p, q, ids: (p, q))
+def update(ids, cmap, front, early, left, right):
+    def where(p, q, ids, cmap):
+        child = sender(ids, 5)
+        return (
+            place(cmap, child, ids[1], p)[0],
+            place(cmap, child, 4 * ids[0] + ids[2], q)[0],
+        )
+
+    tile = pl.BlockSpec((BLK, BLK), lambda p, q, ids, cmap: (p, q))
     return pl.pallas_call(
         update_kernel,
         grid_spec=pltpu.PrefetchScalarGridSpec(
-            num_scalar_prefetch=1,
+            num_scalar_prefetch=2,
             grid=(3, 3),
-            in_specs=[tile]
-            + [pl.BlockSpec((16, 1, 16, PANEL), lambda p, q, ids: (0, p, 0, 0))]
+            in_specs=[tile, pl.BlockSpec((BLK, BLK), where)]
+            + [pl.BlockSpec((16, 1, 16, PANEL), lambda p, q, ids, cmap: (0, p, 0, 0))]
             + [
                 pl.BlockSpec(
-                    (16, 1, 16, PANEL), lambda p, q, ids: (0, jnp.where(p == 0, q, 2), 0, 0)
+                    (16, 1, 16, PANEL), lambda p, q, ids, cmap: (0, jnp.where(p == 0, q, 2), 0, 0)
                 )
             ],
             out_specs=tile,
@@ -209,7 +222,7 @@
         out_shape=jax.ShapeDtypeStruct((3 * BLK, 3 * BLK), F32),
         compiler_params=PARAMS,
         name="update",
-    )(ids, assembled, left, right)
+    )(ids, cmap, front, early, left, right)
 
 
 def finish_kernel(ids, cmap, partial, r0, r1, r2, r3, r4, out):
@@ -258,15 +271,26 @@
     def at(s, r, c):
         return (s * 16 + r) * 4 + c
 
+    ahead = [
+        [(0, 0, 2, (0, 2)), (3, 3, 1, (3, 1)), (1, 2, 1, (2, 1)), (2, 1, 2, (1, 2)), (3, 1, 1, (2, 2)), (0, 2, 2, (1, 1))],
+        [(0, 0, 3, (0, 3)), (3, 3, 0, (3, 0)), (1, 2, 0, (2, 0)), (2, 1, 3, (1, 3))],
+    ]
+    gone = {(s, c, k) for part in ahead for s, c, k, _ in part}
+
     def send(j):
         pairs = []
         for s in range(4):
             for r in range(16):
                 for c in range(4):
-                    group = 4 * c + (s + j) % 4
-                    if (r < 2 or group > 0) and (s, group) not in ((3, 5), (0, 10)):
-                        pairs.append((at(s, r, c), at(c, r, (s + j) % 4)))
+                    k = (s + j) % 4
+                    if (r < 2 or c + k > 0) and (s, c, k) not in gone:
+                        pairs.append((at(s, r, c), at(c, r, k)))
         return lax.ppermute(sent[j], MESH, pairs)
+
+    def send_ahead(block, part):
+        return lax.ppermute(
+            block, MESH, [(at(s, r, c), at(t[0], r, t[1])) for s, c, _, t in part for r in range(16)]
+        )
 
     last = lax.ppermute(front_in[:, :BLK], RING, [(1, 0)])
     sent = masked_groups(ids, pat, child_updates)
@@ -279,12 +303,10 @@
     others = [lax.ppermute(pieces[k], RING, [(4 * s, 4 * s + k) for s in range(4)]) for k in range(1, 4)]
     mine = jnp.where(col == 0, mine, others[0] + others[1] + others[2])
 
-    leg = lax.ppermute(
-        sent[2],
-        MESH,
-        [(at(3, r, 1), at(2, r, 2)) for r in range(16)] + [(at(0, r, 2), at(1, r, 1)) for r in range(16)],
-    )
-    mine, leg = lax.optimization_barrier((mine, leg))
+    leg = send_ahead(jnp.where((sub == 0) | (sub == 3), sent[2], sent[0]), ahead[0])
+    rest = send_ahead(jnp.where(sub < 2, sent[3], sent[1]), ahead[1])
+    mine, leg, rest = lax.optimization_barrier((mine, leg, rest))
+    early = jnp.where(col == jnp.where(sub < 2, 2, 1), leg, rest)
 
     turn = [
         (at(s, r, c), at(r // 4, 4 * s + c, r % 4)) for s in range(4) for r in range(16) for c in range(4)
@@ -302,7 +324,7 @@
         child_map[0, 0] >= 0, spread, lambda turned: jnp.zeros((16,) + turned.shape, F32), turned
     )
     left = lax.all_gather(mine, RING, axis=0)
-    partial = update(ids, front_in, left, right)
+    partial = update(ids, child_map, front_in, early, left, right)
     return finish(ids, child_map, partial, [send(j) for j in range(4)] + [relayed])
 
 

time: 229 us -> 228 us (level)
  the two profiles are of different devices: /device:TPU:31 before, /device:TPU:32 now
where the time goes in v4:
time: 228 us; the launch traced here: 226 us
  waiting for transfers between devices  85.5 us (38%)
  blocking collectives  39.8 us (17%)
  starting transfers between devices  38.5 us (17%)
  Pallas kernels  35.8 us (16%)
  between operations  14.2 us (6%)
  other arithmetic  7.54 us (3%)
  local copies, waits for them, and re-layouts  5.08 us (2%)
    all_to_all x1, blocking collectives, spread(): lax.all_to_all(jnp.broadcast_to(turned, (16,) + turned.shape), 'row', 0, 0)  39.8 us
    ppermute x4, waiting for transfers between devices, send(): return lax.ppermute(sent[j], MESH, pairs)  31.2 us
    ppermute x1, waiting for transfers between devices, shards(): turned = lax.ppermute(mine, MESH, turn)  27.5 us
    ppermute x3, waiting for transfers between devices, shards(): lax.ppermute(pieces[k], RING, [(4 * s, 4 * s + k) for s in range(4)])  26.7 us
    ppermute x4, starting transfers between devices, send(): return lax.ppermute(sent[j], MESH, pairs)  20.5 us
    pallas_call x1, Pallas kernels, update(): pl.pallas_call(update_kernel, grid_spec=pltpu.PrefetchScalarGridSpec(num_...  9.24 us
    pallas_call x1, Pallas kernels, finish(): pl.pallas_call(finish_kernel, grid_spec=pltpu.PrefetchScalarGridSpec(num_...  6.78 us
    ppermute x1, starting transfers between devices, shards(): turned = lax.ppermute(mine, MESH, turn)  6.21 us
  transfers between devices with their start and end apart: 16, of which 4 were waited for; matrix products, arithmetic and copies ran while one was open for 4% of the time, Pallas kernels for 13%

profile of v4, /device:TPU:32, one launch (start us, length us, event | category | flops | bytes accessed | tf_op | source)
XLA Modules:
  0.0 226.5 jit_solution(5298429678069061802)
XLA Ops:
  6.5 1.2 slice.6
  7.7 0.7 collective-permute-start
  8.5 0.6 pad_add_fusion.ids
  9.1 4.4 %masked_groups.1 = (f32[512,512]{1,0:T(8,128)}, f32[512,512]{1,0:T(8,128)}, f32[512,512]{1,0:T(8,128)}, f32[512,512]{1,0:T(8,128)}) custom-call(s32[3]{0:T(128)} %pad_add_fusion.ids, s32[2,8]{1,0:T(2,128)} %bitcast.7, f32[1,512,2048]{2,1,0:T(8,128)} %refs_3_.1, f32[1,512,2048]{2,1,0:T(8,128)} %refs_3_.1, f32[1,512,2048]{2,1,0:T(8,128)} %refs_3_.1, ...), custom_call_target="tpu_custom_call" | custom-call | tf_op jit(solution)/shard_map/masked_groups/pallas_call | solution.py:43
  13.5 1.4 broadcast_select_fusion.1
  14.9 3.3 %collective-permute-start.7 = (f32[512,512]{1,0:T(8,128)S(1)}, f32[512,512]{1,0:T(8,128)}, u32[]{:S(2)}, u32[]{:S(2)}) collective-permute-start(f32[512,512]{1,0:T(8,128)S(1)} %broadcast_select_fusion.1), channel_id=1, source_target_pairs={{0,2},{4,6},{8,10},{12,14},{16,18},{20,22},{24,26},{28,30},{32,34}... | collective-permute-start | bytes 3145736 | tf_op jit(solution)/shard_map/ppermute | solution.py:291
  18.2 0.0 collective-permute-done.last
  18.2 0.0 copy-start
  18.2 0.9 copy-done
  19.1 4.4 %panel_slices.1 = (f32[3,64,1024]{2,1,0:T(8,128)}, f32[3,64,1024]{2,1,0:T(8,128)}, f32[3,64,1024]{2,1,0:T(8,128)}, f32[3,64,1024]{2,1,0:T(8,128)}) custom-call(s32[3]{0:T(128)} %pad_add_fusion.ids, s32[2,8]{1,0:T(2,128)} %bitcast.8, s32[4,32]{1,0:T(4,128)} %cmap.5, f32[1,512,2048]{2,1,0:T(8,128)} %refs_3_.1, f32[768,768]{1,0:T(8,128)} %front.3, ...), custom_call_target="tpu_custom_call" | custom-call | tf_op jit(solution)/shard_map/panel_slices/pallas_call | solution.py:78
  23.5 0.7 collective-permute-start.1
  24.2 0.7 collective-permute-start.2
  24.9 0.7 collective-permute-start.3
  25.6 1.4 broadcast_select_fusion
  27.1 0.7 collective-permute-start.8
  27.8 5.5 %split_pivot.1 = (bf16[1024,1024]{1,0:T(8,128)(2,1)}, bf16[1024,1024]{1,0:T(8,128)(2,1)}) custom-call(f32[1024,1024]{1,0:T(8,128)} %pivot.1), custom_call_target="tpu_custom_call" | custom-call | tf_op jit(solution)/shard_map/split_pivot/pallas_call | solution.py:101
  33.3 0.0 collective-permute-done.1.refs_1_
  33.3 0.0 collective-permute-done.2.refs_2_
  33.4 0.9 copy-done.1
  34.2 0.3 copy-done.2
  34.5 0.3 copy-done.3
  34.8 5.5 %factor_slices.1 = (f32[3,16,1024]{2,1,0:T(8,128)}, f32[3,16,1024]{2,1,0:T(8,128)}, f32[3,16,1024]{2,1,0:T(8,128)}, f32[3,16,1024]{2,1,0:T(8,128)}) custom-call(f32[3,64,1024]{2,1,0:T(8,128)} %get-tuple-element.32.refs_0_, f32[3,64,1024]{2,1,0:T(8,128)} %copy-done.1, f32[3,64,1024]{2,1,0:T(8,128)} %copy-done.2, f32[3,64,1024]{2,1,0:T(8,128)} %copy-done.3, ...), custom_call_target="tpu_custom_call" | custom-call | tf_op jit(solution)/shard_map/factor_slices/pallas_call | solution.py:132
  40.3 0.7 collective-permute-start.4
  41.0 1.3 collective-permute-start.5
  42.3 1.4 collective-permute-start.6
  43.6 0.0 collective-permute-done.4
  43.6 26.6 %collective-permute-done.5 = f32[3,16,1024]{2,1,0:T(8,128)S(1)} collective-permute-done((f32[3,16,1024]{2,1,0:T(8,128)}, f32[3,16,1024]{2,1,0:T(8,128)S(1)}, u32[]{:S(2)}, u32[]{:S(2)}) %collective-permute-start.5) | collective-permute-done | bytes 196640 | tf_op jit(solution)/shard_map/ppermute | solution.py:303
  70.3 0.0 collective-permute-done.6
  70.3 1.6 add_select_fusion
  71.9 0.0 collective-permute-done.7
  71.9 0.0 collective-permute-done.8
  71.9 0.0 all-gather.3.cloned.1.call-update
  72.0 6.2 %collective-permute-start.9 = (f32[3,16,1024]{2,1,0:T(8,128)}, f32[3,16,1024]{2,1,0:T(8,128)S(1)}, u32[]{:S(2)}, u32[]{:S(2)}) collective-permute-start(f32[3,16,1024]{2,1,0:T(8,128)} %add_select_fusion), channel_id=1, source_target_pairs={{0,0},{1,4},{2,8},{3,12},{4,1},{5,5},{6,9},{7,13},{8,2},{9,6},{10,... | collective-permute-start | bytes 589832 | tf_op jit(solution)/shard_map/ppermute | solution.py:314
  78.2 27.5 %collective-permute-done.9 = f32[3,16,1024]{2,1,0:T(8,128)S(1)} collective-permute-done((f32[3,16,1024]{2,1,0:T(8,128)}, f32[3,16,1024]{2,1,0:T(8,128)S(1)}, u32[]{:S(2)}, u32[]{:S(2)}) %collective-permute-start.9) | collective-permute-done | bytes 196640 | tf_op jit(solution)/shard_map/ppermute | solution.py:314
  105.7 1.9 collective-permute-start.10
  107.6 1.9 collective-permute-start.11
  109.6 1.6 collective-permute-start.12
  111.2 15.0 %collective-permute-start.13 = (f32[512,512]{1,0:T(8,128)}, f32[512,512]{1,0:T(8,128)}, u32[]{:S(2)}, u32[]{:S(2)}) collective-permute-start(f32[512,512]{1,0:T(8,128)} %get-tuple-element.53), channel_id=1, source_target_pairs={{1,67},{2,131},{3,195},{5,71},{6,135},{7,199},{9,75},{10,139},{11,... | collective-permute-start | bytes 3145736 | tf_op jit(solution)/shard_map/ppermute | solution.py:288
  126.2 1.7 collective-permute-start.14
  127.9 1.2 slice.7
  129.8 2.4 %broadcast_select_fusion.2.early = f32[512,512]{1,0:T(8,128)} fusion(f32[512,512]{1,0:T(8,128)} %collective-permute-done.7, f32[512,512]{1,0:T(8,128)S(1)} %collective-permute-done.8, pred[]{:T(512)S(6)} %eq.12), kind=kLoop, calls=%fused_computation.2 | loop fusion | flops 262144 | bytes 3145729 | tf_op jit(solution)/shard_map/jit(_where)/select_n | solution.py:309
  132.2 40.2 %conditional.1 = (f32[16,3,16,1024]{3,2,1,0:T(8,128)S(1)}) conditional(s32[]{:T(128)} %bitcast.5, () %tuple.14, f32[3,16,1024]{2,1,0:T(8,128)S(1)} %collective-permute-done.9), branch_computations={%region_0.1_spmd, %region_1.2_spmd} | conditional | bytes 9633800 | solution.py:323
  132.2 0.4 broadcast_in_dim.2
  132.6 39.8 %all_to_all.4 = f32[16,3,16,1024]{3,2,1,0:T(8,128)S(1)} all-to-all(f32[16,3,16,1024]{3,2,1,0:T(8,128)S(1)} %broadcast_in_dim.2), channel_id=1, replica_groups=mesh['sub'=4,'row'=16,'col'=4] {'row'}, dimensions={0} | all-to-all | bytes 6291456 | tf_op jit(solution)/shard_map/cond/branch_1_fun/all_to_all | solution.py:321
  172.4 9.2 %update.1.partial = f32[768,768]{1,0:T(8,128)} custom-call(s32[3]{0:T(128)} %pad_add_fusion.ids, s32[4,32]{1,0:T(4,128)} %cmap.5, f32[768,768]{1,0:T(8,128)} %front.3, f32[512,512]{1,0:T(8,128)} %broadcast_select_fusion.2.early, f32[16,3,16,1024]{3,2,1,0:T(8,128)} %bitcast.6, f32[16,3,16,1024]{3,2,1,0:T(8,128)S(1)} %get-tuple-element.55.refs_1_), custom_call_target="tpu_custom_call" | custom-call | tf_op jit(solution)/shard_map/update/pallas_call | solution.py:202
  181.6 1.4 collective-permute-done.11.r1
  183.0 29.8 %collective-permute-done.13.r3 = f32[512,512]{1,0:T(8,128)} collective-permute-done((f32[512,512]{1,0:T(8,128)}, f32[512,512]{1,0:T(8,128)}, u32[]{:S(2)}, u32[]{:S(2)}) %collective-permute-start.13) | collective-permute-done | bytes 1048608 | tf_op jit(solution)/shard_map/ppermute | solution.py:288
  212.9 6.8 %finish.1 = f32[768,768]{1,0:T(8,128)} custom-call(s32[3]{0:T(128)} %pad_add_fusion.ids, s32[4,32]{1,0:T(4,128)} %cmap.5, f32[768,768]{1,0:T(8,128)} %update.1.partial, f32[512,512]{1,0:T(8,128)} %collective-permute-done.10.r0, f32[512,512]{1,0:T(8,128)} %collective-permute-done.11.r1, f32[512,512]{1,0:T(8,128)} %collective-permute-done.12.r2, ...), custom_call_target="tpu_custom_call" | custom-call | tf_op jit(solution)/shard_map/finish/pallas_call | solution.py:250
  (9 shorter events, 0.0 us)
Async XLA Ops:
  6.5 165.8 %all-gather.3.cloned.1.call-start = ((), (), s32[]{:S(2)}) async-start(), calls=%async_computation.1 | async-start | bytes 3342336 | tf_op jit(solution)/shard_map/all_gather | solution.py:326
  7.7 10.5 %collective-permute-start = (f32[768,256]{1,0:T(8,128)S(1)}, f32[768,256]{1,0:T(8,128)S(1)}, u32[]{:S(2)}, u32[]{:S(2)}) collective-permute-start(f32[768,256]{1,0:T(8,128)S(1)} %slice.6), channel_id=1, source_target_pairs={{1,0},{5,4},{9,8},{13,12},{17,16},{21,20},{25,24},{29,28},{33,32},... | collective-permute-start | bytes 2359304 | tf_op jit(solution)/shard_map/ppermute | solution.py:295
  14.9 57.0 %collective-permute-start.7 = (f32[512,512]{1,0:T(8,128)S(1)}, f32[512,512]{1,0:T(8,128)}, u32[]{:S(2)}, u32[]{:S(2)}) collective-permute-start(f32[512,512]{1,0:T(8,128)S(1)} %broadcast_select_fusion.1), channel_id=1, source_target_pairs={{0,2},{4,6},{8,10},{12,14},{16,18},{20,22},{24,26},{28,30},{32,34}... | collective-permute-start | bytes 3145736 | tf_op jit(solution)/shard_map/ppermute | solution.py:291
  18.2 0.9 copy-start
  23.5 9.8 %collective-permute-start.1 = (f32[3,64,1024]{2,1,0:T(8,128)}, f32[3,64,1024]{2,1,0:T(8,128)S(1)}, u32[]{:S(2)}, u32[]{:S(2)}) collective-permute-start(f32[3,64,1024]{2,1,0:T(8,128)} %get-tuple-element.33), channel_id=1, source_target_pairs={{0,64},{64,128},{128,192},{192,0},{4,68},{68,132},{132,196},{196,4... | collective-permute-start | bytes 2359304 | tf_op jit(solution)/shard_map/ppermute | solution.py:300
  24.2 9.1 %collective-permute-start.2 = (f32[3,64,1024]{2,1,0:T(8,128)}, f32[3,64,1024]{2,1,0:T(8,128)S(1)}, u32[]{:S(2)}, u32[]{:S(2)}) collective-permute-start(f32[3,64,1024]{2,1,0:T(8,128)} %get-tuple-element.34), channel_id=1, source_target_pairs={{0,128},{64,192},{128,0},{192,64},{4,132},{68,196},{132,4},{196,68... | collective-permute-start | bytes 2359304 | tf_op jit(solution)/shard_map/ppermute | solution.py:300
  24.9 8.4 %collective-permute-start.3 = (f32[3,64,1024]{2,1,0:T(8,128)}, f32[3,64,1024]{2,1,0:T(8,128)S(1)}, u32[]{:S(2)}, u32[]{:S(2)}) collective-permute-start(f32[3,64,1024]{2,1,0:T(8,128)} %get-tuple-element.35), channel_id=1, source_target_pairs={{0,192},{64,0},{128,64},{192,128},{4,196},{68,4},{132,68},{196,132... | collective-permute-start | bytes 2359304 | tf_op jit(solution)/shard_map/ppermute | solution.py:300
  27.1 44.9 %collective-permute-start.8 = (f32[512,512]{1,0:T(8,128)S(1)}, f32[512,512]{1,0:T(8,128)S(1)}, u32[]{:S(2)}, u32[]{:S(2)}) collective-permute-start(f32[512,512]{1,0:T(8,128)S(1)} %broadcast_select_fusion), channel_id=1, source_target_pairs={{0,3},{4,7},{8,11},{12,15},{16,19},{20,23},{24,27},{28,31},{32,35}... | collective-permute-start | bytes 3145736 | tf_op jit(solution)/shard_map/ppermute | solution.py:291
  33.3 0.9 copy-start.1
  33.3 1.1 copy-start.2
  33.3 1.5 copy-start.3
  40.3 3.3 %collective-permute-start.4 = (f32[3,16,1024]{2,1,0:T(8,128)}, f32[3,16,1024]{2,1,0:T(8,128)S(1)}, u32[]{:S(2)}, u32[]{:S(2)}) collective-permute-start(f32[3,16,1024]{2,1,0:T(8,128)} %get-tuple-element.39), channel_id=1, source_target_pairs={{0,1},{64,65},{128,129},{192,193},{4,5},{68,69},{132,133},{196,197... | collective-permute-start | bytes 589832 | tf_op jit(solution)/shard_map/ppermute | solution.py:303
  41.0 29.3 %collective-permute-start.5 = (f32[3,16,1024]{2,1,0:T(8,128)}, f32[3,16,1024]{2,1,0:T(8,128)S(1)}, u32[]{:S(2)}, u32[]{:S(2)}) collective-permute-start(f32[3,16,1024]{2,1,0:T(8,128)} %get-tuple-element.40), channel_id=1, source_target_pairs={{0,2},{64,66},{128,130},{192,194},{4,6},{68,70},{132,134},{196,198... | collective-permute-start | bytes 589832 | tf_op jit(solution)/shard_map/ppermute | solution.py:303
  42.3 28.0 %collective-permute-start.6 = (f32[3,16,1024]{2,1,0:T(8,128)}, f32[3,16,1024]{2,1,0:T(8,128)}, u32[]{:S(2)}, u32[]{:S(2)}) collective-permute-start(f32[3,16,1024]{2,1,0:T(8,128)} %get-tuple-element.41), channel_id=1, source_target_pairs={{0,3},{64,67},{128,131},{192,195},{4,7},{68,71},{132,135},{196,199... | collective-permute-start | bytes 589832 | tf_op jit(solution)/shard_map/ppermute | solution.py:303
  72.0 33.8 %collective-permute-start.9 = (f32[3,16,1024]{2,1,0:T(8,128)}, f32[3,16,1024]{2,1,0:T(8,128)S(1)}, u32[]{:S(2)}, u32[]{:S(2)}) collective-permute-start(f32[3,16,1024]{2,1,0:T(8,128)} %add_select_fusion), channel_id=1, source_target_pairs={{0,0},{1,4},{2,8},{3,12},{4,1},{5,5},{6,9},{7,13},{8,2},{9,6},{10,... | collective-permute-start | bytes 589832 | tf_op jit(solution)/shard_map/ppermute | solution.py:314
  105.7 75.9 %collective-permute-start.10 = (f32[512,512]{1,0:T(8,128)}, f32[512,512]{1,0:T(8,128)}, u32[]{:S(2)}, u32[]{:S(2)}) collective-permute-start(f32[512,512]{1,0:T(8,128)} %get-tuple-element.50), channel_id=1, source_target_pairs={{0,0},{1,64},{2,128},{3,192},{4,4},{5,68},{6,132},{7,196},{9,72},{... | collective-permute-start | bytes 3145736 | tf_op jit(solution)/shard_map/ppermute | solution.py:288
  107.6 75.4 %collective-permute-start.11 = (f32[512,512]{1,0:T(8,128)}, f32[512,512]{1,0:T(8,128)}, u32[]{:S(2)}, u32[]{:S(2)}) collective-permute-start(f32[512,512]{1,0:T(8,128)} %get-tuple-element.51), channel_id=1, source_target_pairs={{0,1},{1,65},{2,129},{3,193},{4,5},{5,69},{6,133},{7,197},{8,9},{9... | collective-permute-start | bytes 3145736 | tf_op jit(solution)/shard_map/ppermute | solution.py:288
  109.6 73.4 %collective-permute-start.12 = (f32[512,512]{1,0:T(8,128)}, f32[512,512]{1,0:T(8,128)}, u32[]{:S(2)}, u32[]{:S(2)}) collective-permute-start(f32[512,512]{1,0:T(8,128)} %get-tuple-element.52), channel_id=1, source_target_pairs={{1,66},{3,194},{5,70},{7,198},{9,74},{11,202},{13,78},{15,206},{17... | collective-permute-start | bytes 3145736 | tf_op jit(solution)/shard_map/ppermute | solution.py:288
  111.2 101.6 %collective-permute-start.13 = (f32[512,512]{1,0:T(8,128)}, f32[512,512]{1,0:T(8,128)}, u32[]{:S(2)}, u32[]{:S(2)}) collective-permute-start(f32[512,512]{1,0:T(8,128)} %get-tuple-element.53), channel_id=1, source_target_pairs={{1,67},{2,131},{3,195},{5,71},{6,135},{7,199},{9,75},{10,139},{11,... | collective-permute-start | bytes 3145736 | tf_op jit(solution)/shard_map/ppermute | solution.py:288
  126.2 86.6 %collective-permute-start.14 = (f32[512,512]{1,0:T(8,128)}, f32[512,512]{1,0:T(8,128)}, u32[]{:S(2)}, u32[]{:S(2)}) collective-permute-start(f32[512,512]{1,0:T(8,128)} %collective-permute-done.7), channel_id=1, source_target_pairs={{65,130},{69,134},{73,138},{77,142},{81,146},{85,150},{89,154},{93... | collective-permute-start | bytes 3145736 | tf_op jit(solution)/shard_map/ppermute | solution.py:316
Sparse Core Ops, SparseCore 0:
  72.1 64.8 all-gather.2

commit v5 on v4

--- a/solution.py
+++ b/solution.py
@@ -305,17 +305,18 @@
 
     leg = send_ahead(jnp.where((sub == 0) | (sub == 3), sent[2], sent[0]), ahead[0])
     rest = send_ahead(jnp.where(sub < 2, sent[3], sent[1]), ahead[1])
-    mine, leg, rest = lax.optimization_barrier((mine, leg, rest))
+    mine, leg, rest, sent = lax.optimization_barrier((mine, leg, rest, sent))
+    relayed = lax.ppermute(
+        leg, MESH, [(at(s, r, s), at(3 - s, r, 3 - s)) for s in (1, 2) for r in range(16)]
+    )
+    arrived = {j: send(j) for j in (0, 1, 2)}
     early = jnp.where(col == jnp.where(sub < 2, 2, 1), leg, rest)
 
     turn = [
         (at(s, r, c), at(r // 4, 4 * s + c, r % 4)) for s in range(4) for r in range(16) for c in range(4)
     ]
     turned = lax.ppermute(mine, MESH, turn)
-    turned, sent, leg = lax.optimization_barrier((turned, sent, leg))
-    relayed = lax.ppermute(
-        leg, MESH, [(at(s, r, s), at(3 - s, r, 3 - s)) for s in (1, 2) for r in range(16)]
-    )
+    turned, sent = lax.optimization_barrier((turned, sent))
 
     def spread(turned):
         return lax.all_to_all(jnp.broadcast_to(turned, (16,) + turned.shape), "row", 0, 0)
@@ -325,7 +326,7 @@
     )
     left = lax.all_gather(mine, RING, axis=0)
     partial = update(ids, child_map, front_in, early, left, right)
-    return finish(ids, child_map, partial, [send(j) for j in range(4)] + [relayed])
+    return finish(ids, child_map, partial, [arrived[j] if j in arrived else send(j) for j in range(4)] + [relayed])
 
 
 def solution(mesh):

time: 228 us -> 227 us (level)
    ppermute x4, waiting for transfers between devices: 31.2 us -> 50.2 us  [send(): return lax.ppermute(sent[j], MESH, pairs)]
    ppermute x1, waiting for transfers between devices: 27.5 us -> 8.66 us  [shards(): turned = lax.ppermute(mine, MESH, turn)]
  transfers between devices with their start and end apart: 16 -> 16, of which waited for: 4 -> 5; matrix products, arithmetic and copies ran while one was open for 4% -> 4% of each run, Pallas kernels for 13% -> 13%
where the time goes in v5:
time: 227 us; the launch traced here: 226 us
  waiting for transfers between devices  85.6 us (38%)
  blocking collectives  40.2 us (18%)
  starting transfers between devices  37.2 us (16%)
  Pallas kernels  35.8 us (16%)
  between operations  14.2 us (6%)
  other arithmetic  7.54 us (3%)
  local copies, waits for them, and re-layouts  5.08 us (2%)
    ppermute x4, waiting for transfers between devices, send(): return lax.ppermute(sent[j], MESH, pairs)  50.2 us
    all_to_all x1, blocking collectives, spread(): lax.all_to_all(jnp.broadcast_to(turned, (16,) + turned.shape), 'row', 0, 0)  40.2 us
    ppermute x3, waiting for transfers between devices, shards(): lax.ppermute(pieces[k], RING, [(4 * s, 4 * s + k) for s in range(4)])  26.6 us
    ppermute x4, starting transfers between devices, send(): return lax.ppermute(sent[j], MESH, pairs)  19.2 us
    pallas_call x1, Pallas kernels, update(): pl.pallas_call(update_kernel, grid_spec=pltpu.PrefetchScalarGridSpec(num_...  9.24 us
    ppermute x1, waiting for transfers between devices, shards(): turned = lax.ppermute(mine, MESH, turn)  8.66 us
    pallas_call x1, Pallas kernels, finish(): pl.pallas_call(finish_kernel, grid_spec=pltpu.PrefetchScalarGridSpec(num_...  6.81 us
    ppermute x1, starting transfers between devices, shards(): turned = lax.ppermute(mine, MESH, turn)  6.21 us
  transfers between devices with their start and end apart: 16, of which 5 were waited for; matrix products, arithmetic and copies ran while one was open for 4% of the time, Pallas kernels for 13%

profile of v5, /device:TPU:32, one launch (start us, length us, event | category | flops | bytes accessed | tf_op | source)
XLA Modules:
  0.0 225.7 jit_solution(6753443577364225073)
XLA Ops:
  6.5 1.2 slice.6
  7.7 0.7 collective-permute-start
  8.5 0.6 pad_add_fusion.ids
  9.1 4.4 %masked_groups.1 = (f32[512,512]{1,0:T(8,128)}, f32[512,512]{1,0:T(8,128)}, f32[512,512]{1,0:T(8,128)}, f32[512,512]{1,0:T(8,128)}) custom-call(s32[3]{0:T(128)} %pad_add_fusion.ids, s32[2,8]{1,0:T(2,128)} %bitcast.7, f32[1,512,2048]{2,1,0:T(8,128)} %refs_3_.1, f32[1,512,2048]{2,1,0:T(8,128)} %refs_3_.1, f32[1,512,2048]{2,1,0:T(8,128)} %refs_3_.1, ...), custom_call_target="tpu_custom_call" | custom-call | tf_op jit(solution)/shard_map/masked_groups/pallas_call | solution.py:43
  13.5 1.4 broadcast_select_fusion.1
  14.9 3.3 %collective-permute-start.7 = (f32[512,512]{1,0:T(8,128)S(1)}, f32[512,512]{1,0:T(8,128)}, u32[]{:S(2)}, u32[]{:S(2)}) collective-permute-start(f32[512,512]{1,0:T(8,128)S(1)} %broadcast_select_fusion.1), channel_id=1, source_target_pairs={{0,2},{4,6},{8,10},{12,14},{16,18},{20,22},{24,26},{28,30},{32,34}... | collective-permute-start | bytes 3145736 | tf_op jit(solution)/shard_map/ppermute | solution.py:291
  18.2 0.0 collective-permute-done.last
  18.2 0.0 copy-start
  18.2 0.9 copy-done
  19.1 4.4 %panel_slices.1 = (f32[3,64,1024]{2,1,0:T(8,128)}, f32[3,64,1024]{2,1,0:T(8,128)}, f32[3,64,1024]{2,1,0:T(8,128)}, f32[3,64,1024]{2,1,0:T(8,128)}) custom-call(s32[3]{0:T(128)} %pad_add_fusion.ids, s32[2,8]{1,0:T(2,128)} %bitcast.8, s32[4,32]{1,0:T(4,128)} %cmap.5, f32[1,512,2048]{2,1,0:T(8,128)} %refs_3_.1, f32[768,768]{1,0:T(8,128)} %front.3, ...), custom_call_target="tpu_custom_call" | custom-call | tf_op jit(solution)/shard_map/panel_slices/pallas_call | solution.py:78
  23.4 0.7 collective-permute-start.1
  24.1 0.7 collective-permute-start.2
  24.9 0.7 collective-permute-start.3
  25.6 1.4 broadcast_select_fusion
  27.0 0.7 collective-permute-start.8
  27.8 5.5 %split_pivot.1 = (bf16[1024,1024]{1,0:T(8,128)(2,1)}, bf16[1024,1024]{1,0:T(8,128)(2,1)}) custom-call(f32[1024,1024]{1,0:T(8,128)} %pivot.1), custom_call_target="tpu_custom_call" | custom-call | tf_op jit(solution)/shard_map/split_pivot/pallas_call | solution.py:101
  33.3 0.0 collective-permute-done.1.refs_1_
  33.3 0.0 collective-permute-done.3.refs_3_
  33.3 0.9 copy-done.1
  34.2 0.3 copy-done.2
  34.4 0.3 copy-done.3
  34.7 5.5 %factor_slices.1 = (f32[3,16,1024]{2,1,0:T(8,128)}, f32[3,16,1024]{2,1,0:T(8,128)}, f32[3,16,1024]{2,1,0:T(8,128)}, f32[3,16,1024]{2,1,0:T(8,128)}) custom-call(f32[3,64,1024]{2,1,0:T(8,128)} %get-tuple-element.32.refs_0_, f32[3,64,1024]{2,1,0:T(8,128)} %copy-done.1, f32[3,64,1024]{2,1,0:T(8,128)} %copy-done.2, f32[3,64,1024]{2,1,0:T(8,128)} %copy-done.3, ...), custom_call_target="tpu_custom_call" | custom-call | tf_op jit(solution)/shard_map/factor_slices/pallas_call | solution.py:132
  40.3 0.7 collective-permute-start.4
  40.9 1.3 collective-permute-start.5
  42.2 1.4 collective-permute-start.6
  43.6 0.0 collective-permute-done.4
  43.6 26.6 %collective-permute-done.5 = f32[3,16,1024]{2,1,0:T(8,128)S(1)} collective-permute-done((f32[3,16,1024]{2,1,0:T(8,128)}, f32[3,16,1024]{2,1,0:T(8,128)S(1)}, u32[]{:S(2)}, u32[]{:S(2)}) %collective-permute-start.5) | collective-permute-done | bytes 196640 | tf_op jit(solution)/shard_map/ppermute | solution.py:303
  70.2 1.6 add_select_fusion
  71.9 0.0 collective-permute-done.7
  71.9 0.0 all-gather.3.cloned.1.call-update
  71.9 6.2 %collective-permute-start.9 = (f32[3,16,1024]{2,1,0:T(8,128)}, f32[3,16,1024]{2,1,0:T(8,128)S(1)}, u32[]{:S(2)}, u32[]{:S(2)}) collective-permute-start(f32[3,16,1024]{2,1,0:T(8,128)} %add_select_fusion), channel_id=1, source_target_pairs={{0,0},{1,4},{2,8},{3,12},{4,1},{5,5},{6,9},{7,13},{8,2},{9,6},{10,... | collective-permute-start | bytes 589832 | tf_op jit(solution)/shard_map/ppermute | solution.py:318
  78.1 6.6 %collective-permute-start.10 = (f32[512,512]{1,0:T(8,128)}, f32[512,512]{1,0:T(8,128)}, u32[]{:S(2)}, u32[]{:S(2)}) collective-permute-start(f32[512,512]{1,0:T(8,128)} %get-tuple-element.49), channel_id=1, source_target_pairs={{0,0},{1,64},{2,128},{3,192},{4,4},{5,68},{6,132},{7,196},{9,72},{... | collective-permute-start | bytes 3145736 | tf_op jit(solution)/shard_map/ppermute | solution.py:288
  84.7 2.3 %collective-permute-start.11 = (f32[512,512]{1,0:T(8,128)}, f32[512,512]{1,0:T(8,128)}, u32[]{:S(2)}, u32[]{:S(2)}) collective-permute-start(f32[512,512]{1,0:T(8,128)} %get-tuple-element.50), channel_id=1, source_target_pairs={{0,1},{1,65},{2,129},{3,193},{4,5},{5,69},{6,133},{7,197},{8,9},{9... | collective-permute-start | bytes 3145736 | tf_op jit(solution)/shard_map/ppermute | solution.py:288
  87.0 1.6 collective-permute-start.12
  88.6 1.7 collective-permute-start.14
  90.3 8.7 %collective-permute-done.9 = f32[3,16,1024]{2,1,0:T(8,128)S(1)} collective-permute-done((f32[3,16,1024]{2,1,0:T(8,128)}, f32[3,16,1024]{2,1,0:T(8,128)S(1)}, u32[]{:S(2)}, u32[]{:S(2)}) %collective-permute-start.9) | collective-permute-done | bytes 196640 | tf_op jit(solution)/shard_map/ppermute | solution.py:318
  98.9 8.8 %collective-permute-start.13 = (f32[512,512]{1,0:T(8,128)}, f32[512,512]{1,0:T(8,128)}, u32[]{:S(2)}, u32[]{:S(2)}) collective-permute-start(f32[512,512]{1,0:T(8,128)} %get-tuple-element.54), channel_id=1, source_target_pairs={{1,67},{2,131},{3,195},{5,71},{6,135},{7,199},{9,75},{10,139},{11,... | collective-permute-start | bytes 3145736 | tf_op jit(solution)/shard_map/ppermute | solution.py:288
  107.7 1.2 slice.7
  109.6 2.4 %broadcast_select_fusion.2.early = f32[512,512]{1,0:T(8,128)} fusion(f32[512,512]{1,0:T(8,128)} %collective-permute-done.7, f32[512,512]{1,0:T(8,128)S(1)} %collective-permute-done.8, pred[]{:T(512)S(6)} %eq.12), kind=kLoop, calls=%fused_computation.2 | loop fusion | flops 262144 | bytes 3145729 | tf_op jit(solution)/shard_map/jit(_where)/select_n | solution.py:313
  112.0 40.6 %conditional.1 = (f32[16,3,16,1024]{3,2,1,0:T(8,128)S(1)}) conditional(s32[]{:T(128)} %bitcast.5, () %tuple.14, f32[3,16,1024]{2,1,0:T(8,128)S(1)} %collective-permute-done.9), branch_computations={%region_0.1_spmd, %region_1.2_spmd} | conditional | bytes 9633800 | solution.py:324
  112.0 0.4 broadcast_in_dim.2
  112.4 40.2 %all_to_all.4 = f32[16,3,16,1024]{3,2,1,0:T(8,128)S(1)} all-to-all(f32[16,3,16,1024]{3,2,1,0:T(8,128)S(1)} %broadcast_in_dim.2), channel_id=1, replica_groups=mesh['sub'=4,'row'=16,'col'=4] {'row'}, dimensions={0} | all-to-all | bytes 6291456 | tf_op jit(solution)/shard_map/cond/branch_1_fun/all_to_all | solution.py:322
  152.6 9.2 %update.1.partial = f32[768,768]{1,0:T(8,128)} custom-call(s32[3]{0:T(128)} %pad_add_fusion.ids, s32[4,32]{1,0:T(4,128)} %cmap.5, f32[768,768]{1,0:T(8,128)} %front.3, f32[512,512]{1,0:T(8,128)} %broadcast_select_fusion.2.early, f32[16,3,16,1024]{3,2,1,0:T(8,128)} %bitcast.6, f32[16,3,16,1024]{3,2,1,0:T(8,128)S(1)} %get-tuple-element.55.refs_1_), custom_call_target="tpu_custom_call" | custom-call | tf_op jit(solution)/shard_map/update/pallas_call | solution.py:202
  161.8 1.1 collective-permute-done.10.r0
  162.9 12.4 %collective-permute-done.11.r1 = f32[512,512]{1,0:T(8,128)} collective-permute-done((f32[512,512]{1,0:T(8,128)}, f32[512,512]{1,0:T(8,128)}, u32[]{:S(2)}, u32[]{:S(2)}) %collective-permute-start.11) | collective-permute-done | bytes 1048608 | tf_op jit(solution)/shard_map/ppermute | solution.py:288
  175.3 0.0 collective-permute-done.14.r4
  175.3 36.8 %collective-permute-done.13.r3 = f32[512,512]{1,0:T(8,128)} collective-permute-done((f32[512,512]{1,0:T(8,128)}, f32[512,512]{1,0:T(8,128)}, u32[]{:S(2)}, u32[]{:S(2)}) %collective-permute-start.13) | collective-permute-done | bytes 1048608 | tf_op jit(solution)/shard_map/ppermute | solution.py:288
  212.1 6.8 %finish.1 = f32[768,768]{1,0:T(8,128)} custom-call(s32[3]{0:T(128)} %pad_add_fusion.ids, s32[4,32]{1,0:T(4,128)} %cmap.5, f32[768,768]{1,0:T(8,128)} %update.1.partial, f32[512,512]{1,0:T(8,128)} %collective-permute-done.10.r0, f32[512,512]{1,0:T(8,128)} %collective-permute-done.11.r1, f32[512,512]{1,0:T(8,128)} %collective-permute-done.12.r2, ...), custom_call_target="tpu_custom_call" | custom-call | tf_op jit(solution)/shard_map/finish/pallas_call | solution.py:250
  (9 shorter events, 0.0 us)
Async XLA Ops:
  6.5 146.1 %all-gather.3.cloned.1.call-start = ((), (), s32[]{:S(2)}) async-start(), calls=%async_computation.1 | async-start | bytes 3342336 | tf_op jit(solution)/shard_map/all_gather | solution.py:327
  7.7 10.5 %collective-permute-start = (f32[768,256]{1,0:T(8,128)S(1)}, f32[768,256]{1,0:T(8,128)S(1)}, u32[]{:S(2)}, u32[]{:S(2)}) collective-permute-start(f32[768,256]{1,0:T(8,128)S(1)} %slice.6), channel_id=1, source_target_pairs={{1,0},{5,4},{9,8},{13,12},{17,16},{21,20},{25,24},{29,28},{33,32},... | collective-permute-start | bytes 2359304 | tf_op jit(solution)/shard_map/ppermute | solution.py:295
  14.9 57.0 %collective-permute-start.7 = (f32[512,512]{1,0:T(8,128)S(1)}, f32[512,512]{1,0:T(8,128)}, u32[]{:S(2)}, u32[]{:S(2)}) collective-permute-start(f32[512,512]{1,0:T(8,128)S(1)} %broadcast_select_fusion.1), channel_id=1, source_target_pairs={{0,2},{4,6},{8,10},{12,14},{16,18},{20,22},{24,26},{28,30},{32,34}... | collective-permute-start | bytes 3145736 | tf_op jit(solution)/shard_map/ppermute | solution.py:291
  18.2 0.9 copy-start
  23.4 9.8 %collective-permute-start.1 = (f32[3,64,1024]{2,1,0:T(8,128)}, f32[3,64,1024]{2,1,0:T(8,128)S(1)}, u32[]{:S(2)}, u32[]{:S(2)}) collective-permute-start(f32[3,64,1024]{2,1,0:T(8,128)} %get-tuple-element.33), channel_id=1, source_target_pairs={{0,64},{64,128},{128,192},{192,0},{4,68},{68,132},{132,196},{196,4... | collective-permute-start | bytes 2359304 | tf_op jit(solution)/shard_map/ppermute | solution.py:300
  24.1 9.1 %collective-permute-start.2 = (f32[3,64,1024]{2,1,0:T(8,128)}, f32[3,64,1024]{2,1,0:T(8,128)S(1)}, u32[]{:S(2)}, u32[]{:S(2)}) collective-permute-start(f32[3,64,1024]{2,1,0:T(8,128)} %get-tuple-element.34), channel_id=1, source_target_pairs={{0,128},{64,192},{128,0},{192,64},{4,132},{68,196},{132,4},{196,68... | collective-permute-start | bytes 2359304 | tf_op jit(solution)/shard_map/ppermute | solution.py:300
  24.9 8.4 %collective-permute-start.3 = (f32[3,64,1024]{2,1,0:T(8,128)}, f32[3,64,1024]{2,1,0:T(8,128)S(1)}, u32[]{:S(2)}, u32[]{:S(2)}) collective-permute-start(f32[3,64,1024]{2,1,0:T(8,128)} %get-tuple-element.35), channel_id=1, source_target_pairs={{0,192},{64,0},{128,64},{192,128},{4,196},{68,4},{132,68},{196,132... | collective-permute-start | bytes 2359304 | tf_op jit(solution)/shard_map/ppermute | solution.py:300
  27.0 44.9 %collective-permute-start.8 = (f32[512,512]{1,0:T(8,128)S(1)}, f32[512,512]{1,0:T(8,128)S(1)}, u32[]{:S(2)}, u32[]{:S(2)}) collective-permute-start(f32[512,512]{1,0:T(8,128)S(1)} %broadcast_select_fusion), channel_id=1, source_target_pairs={{0,3},{4,7},{8,11},{12,15},{16,19},{20,23},{24,27},{28,31},{32,35}... | collective-permute-start | bytes 3145736 | tf_op jit(solution)/shard_map/ppermute | solution.py:291
  33.3 0.9 copy-start.1
  33.3 1.1 copy-start.2
  33.3 1.5 copy-start.3
  40.3 3.3 %collective-permute-start.4 = (f32[3,16,1024]{2,1,0:T(8,128)}, f32[3,16,1024]{2,1,0:T(8,128)S(1)}, u32[]{:S(2)}, u32[]{:S(2)}) collective-permute-start(f32[3,16,1024]{2,1,0:T(8,128)} %get-tuple-element.39), channel_id=1, source_target_pairs={{0,1},{64,65},{128,129},{192,193},{4,5},{68,69},{132,133},{196,197... | collective-permute-start | bytes 589832 | tf_op jit(solution)/shard_map/ppermute | solution.py:303
  40.9 29.3 %collective-permute-start.5 = (f32[3,16,1024]{2,1,0:T(8,128)}, f32[3,16,1024]{2,1,0:T(8,128)S(1)}, u32[]{:S(2)}, u32[]{:S(2)}) collective-permute-start(f32[3,16,1024]{2,1,0:T(8,128)} %get-tuple-element.40), channel_id=1, source_target_pairs={{0,2},{64,66},{128,130},{192,194},{4,6},{68,70},{132,134},{196,198... | collective-permute-start | bytes 589832 | tf_op jit(solution)/shard_map/ppermute | solution.py:303
  42.2 28.0 %collective-permute-start.6 = (f32[3,16,1024]{2,1,0:T(8,128)}, f32[3,16,1024]{2,1,0:T(8,128)}, u32[]{:S(2)}, u32[]{:S(2)}) collective-permute-start(f32[3,16,1024]{2,1,0:T(8,128)} %get-tuple-element.41), channel_id=1, source_target_pairs={{0,3},{64,67},{128,131},{192,195},{4,7},{68,71},{132,135},{196,199... | collective-permute-start | bytes 589832 | tf_op jit(solution)/shard_map/ppermute | solution.py:303
  71.9 27.0 %collective-permute-start.9 = (f32[3,16,1024]{2,1,0:T(8,128)}, f32[3,16,1024]{2,1,0:T(8,128)S(1)}, u32[]{:S(2)}, u32[]{:S(2)}) collective-permute-start(f32[3,16,1024]{2,1,0:T(8,128)} %add_select_fusion), channel_id=1, source_target_pairs={{0,0},{1,4},{2,8},{3,12},{4,1},{5,5},{6,9},{7,13},{8,2},{9,6},{10,... | collective-permute-start | bytes 589832 | tf_op jit(solution)/shard_map/ppermute | solution.py:318
  78.1 84.8 %collective-permute-start.10 = (f32[512,512]{1,0:T(8,128)}, f32[512,512]{1,0:T(8,128)}, u32[]{:S(2)}, u32[]{:S(2)}) collective-permute-start(f32[512,512]{1,0:T(8,128)} %get-tuple-element.49), channel_id=1, source_target_pairs={{0,0},{1,64},{2,128},{3,192},{4,4},{5,68},{6,132},{7,196},{9,72},{... | collective-permute-start | bytes 3145736 | tf_op jit(solution)/shard_map/ppermute | solution.py:288
  84.7 90.6 %collective-permute-start.11 = (f32[512,512]{1,0:T(8,128)}, f32[512,512]{1,0:T(8,128)}, u32[]{:S(2)}, u32[]{:S(2)}) collective-permute-start(f32[512,512]{1,0:T(8,128)} %get-tuple-element.50), channel_id=1, source_target_pairs={{0,1},{1,65},{2,129},{3,193},{4,5},{5,69},{6,133},{7,197},{8,9},{9... | collective-permute-start | bytes 3145736 | tf_op jit(solution)/shard_map/ppermute | solution.py:288
  87.0 88.3 %collective-permute-start.12 = (f32[512,512]{1,0:T(8,128)}, f32[512,512]{1,0:T(8,128)}, u32[]{:S(2)}, u32[]{:S(2)}) collective-permute-start(f32[512,512]{1,0:T(8,128)} %get-tuple-element.51), channel_id=1, source_target_pairs={{1,66},{3,194},{5,70},{7,198},{9,74},{11,202},{13,78},{15,206},{17... | collective-permute-start | bytes 3145736 | tf_op jit(solution)/shard_map/ppermute | solution.py:288
  88.6 86.7 %collective-permute-start.14 = (f32[512,512]{1,0:T(8,128)}, f32[512,512]{1,0:T(8,128)}, u32[]{:S(2)}, u32[]{:S(2)}) collective-permute-start(f32[512,512]{1,0:T(8,128)} %collective-permute-done.7), channel_id=1, source_target_pairs={{65,130},{69,134},{73,138},{77,142},{81,146},{85,150},{89,154},{93... | collective-permute-start | bytes 3145736 | tf_op jit(solution)/shard_map/ppermute | solution.py:309
  98.9 113.2 %collective-permute-start.13 = (f32[512,512]{1,0:T(8,128)}, f32[512,512]{1,0:T(8,128)}, u32[]{:S(2)}, u32[]{:S(2)}) collective-permute-start(f32[512,512]{1,0:T(8,128)} %get-tuple-element.54), channel_id=1, source_target_pairs={{1,67},{2,131},{3,195},{5,71},{6,135},{7,199},{9,75},{10,139},{11,... | collective-permute-start | bytes 3145736 | tf_op jit(solution)/shard_map/ppermute | solution.py:288
Sparse Core Ops, SparseCore 0:
  72.0 67.3 all-gather.2

commit v6 on v5

--- a/solution.py
+++ b/solution.py
@@ -226,7 +226,7 @@
 
 
 def finish_kernel(ids, cmap, partial, r0, r1, r2, r3, r4, out):
-    p = pl.program_id(0)
+    p = pl.program_id(0) // 2
     group = 4 * ids[0] + ids[2]
     for q in range(3):
         cols = pl.ds(q * BLK, BLK)
@@ -243,15 +243,16 @@
 def finish(ids, cmap, partial, arrived):
     def arrival(j):
         return pl.BlockSpec(
-            (BLK, 2 * BLK), lambda p, ids, cmap: (place(cmap, sender(ids, j), ids[1], p)[0], 0)
+            (BLK // 2, 2 * BLK),
+            lambda i, ids, cmap: (2 * place(cmap, sender(ids, j), ids[1], i // 2)[0] + i % 2, 0),
         )
 
-    band = pl.BlockSpec((BLK, 3 * BLK), lambda p, ids, cmap: (p, 0))
+    band = pl.BlockSpec((BLK // 2, 3 * BLK), lambda i, ids, cmap: (i, 0))
     return pl.pallas_call(
         finish_kernel,
         grid_spec=pltpu.PrefetchScalarGridSpec(
             num_scalar_prefetch=2,
-            grid=(3,),
+            grid=(6,),
             in_specs=[band] + [arrival(j) for j in (0, 1, 2, 3, 2)],
             out_specs=band,
         ),

time: 227 us -> 228 us (level)
  no operation moved by 1% of the time
where the time goes in v6:
time: 228 us; the launch traced here: 227 us
  waiting for transfers between devices  85.4 us (37%)
  blocking collectives  40.6 us (18%)
  starting transfers between devices  37 us (16%)
  Pallas kernels  36.6 us (16%)
  between operations  14.2 us (6%)
  other arithmetic  7.54 us (3%)
  local copies, waits for them, and re-layouts  5.08 us (2%)
    ppermute x4, waiting for transfers between devices, send(): return lax.ppermute(sent[j], MESH, pairs)  50.1 us
    all_to_all x1, blocking collectives, spread(): lax.all_to_all(jnp.broadcast_to(turned, (16,) + turned.shape), 'row', 0, 0)  40.6 us
    ppermute x3, waiting for transfers between devices, shards(): lax.ppermute(pieces[k], RING, [(4 * s, 4 * s + k) for s in range(4)])  26.6 us
    ppermute x4, starting transfers between devices, send(): return lax.ppermute(sent[j], MESH, pairs)  19 us
    pallas_call x1, Pallas kernels, update(): pl.pallas_call(update_kernel, grid_spec=pltpu.PrefetchScalarGridSpec(num_...  9.24 us
    ppermute x1, waiting for transfers between devices, shards(): turned = lax.ppermute(mine, MESH, turn)  8.66 us
    pallas_call x1, Pallas kernels, finish(): pl.pallas_call(finish_kernel, grid_spec=pltpu.PrefetchScalarGridSpec(num_...  7.59 us
    ppermute x1, starting transfers between devices, shards(): turned = lax.ppermute(mine, MESH, turn)  6.21 us
  transfers between devices with their start and end apart: 16, of which 5 were waited for; matrix products, arithmetic and copies ran while one was open for 4% of the time, Pallas kernels for 13%

profile of v6, /device:TPU:32, one launch (start us, length us, event | category | flops | bytes accessed | tf_op | source)
XLA Modules:
  0.0 226.5 jit_solution(6025022936523569571)
XLA Ops:
  6.5 1.2 slice.6
  7.7 0.7 collective-permute-start
  8.5 0.6 pad_add_fusion.ids
  9.1 4.4 %masked_groups.1 = (f32[512,512]{1,0:T(8,128)}, f32[512,512]{1,0:T(8,128)}, f32[512,512]{1,0:T(8,128)}, f32[512,512]{1,0:T(8,128)}) custom-call(s32[3]{0:T(128)} %pad_add_fusion.ids, s32[2,8]{1,0:T(2,128)} %bitcast.7, f32[1,512,2048]{2,1,0:T(8,128)} %refs_3_.1, f32[1,512,2048]{2,1,0:T(8,128)} %refs_3_.1, f32[1,512,2048]{2,1,0:T(8,128)} %refs_3_.1, ...), custom_call_target="tpu_custom_call" | custom-call | tf_op jit(solution)/shard_map/masked_groups/pallas_call | solution.py:43
  13.5 1.4 broadcast_select_fusion.1
  14.9 3.3 %collective-permute-start.7 = (f32[512,512]{1,0:T(8,128)S(1)}, f32[512,512]{1,0:T(8,128)}, u32[]{:S(2)}, u32[]{:S(2)}) collective-permute-start(f32[512,512]{1,0:T(8,128)S(1)} %broadcast_select_fusion.1), channel_id=1, source_target_pairs={{0,2},{4,6},{8,10},{12,14},{16,18},{20,22},{24,26},{28,30},{32,34}... | collective-permute-start | bytes 3145736 | tf_op jit(solution)/shard_map/ppermute | solution.py:292
  18.2 0.0 collective-permute-done.last
  18.2 0.0 copy-start
  18.2 0.9 copy-done
  19.1 4.4 %panel_slices.1 = (f32[3,64,1024]{2,1,0:T(8,128)}, f32[3,64,1024]{2,1,0:T(8,128)}, f32[3,64,1024]{2,1,0:T(8,128)}, f32[3,64,1024]{2,1,0:T(8,128)}) custom-call(s32[3]{0:T(128)} %pad_add_fusion.ids, s32[2,8]{1,0:T(2,128)} %bitcast.8, s32[4,32]{1,0:T(4,128)} %cmap.5, f32[1,512,2048]{2,1,0:T(8,128)} %refs_3_.1, f32[768,768]{1,0:T(8,128)} %front.3, ...), custom_call_target="tpu_custom_call" | custom-call | tf_op jit(solution)/shard_map/panel_slices/pallas_call | solution.py:78
  23.4 0.7 collective-permute-start.1
  24.1 0.7 collective-permute-start.2
  24.9 0.7 collective-permute-start.3
  25.6 1.4 broadcast_select_fusion
  27.0 0.7 collective-permute-start.8
  27.8 5.5 %split_pivot.1 = (bf16[1024,1024]{1,0:T(8,128)(2,1)}, bf16[1024,1024]{1,0:T(8,128)(2,1)}) custom-call(f32[1024,1024]{1,0:T(8,128)} %pivot.1), custom_call_target="tpu_custom_call" | custom-call | tf_op jit(solution)/shard_map/split_pivot/pallas_call | solution.py:101
  33.3 0.0 collective-permute-done.1.refs_1_
  33.3 0.0 collective-permute-done.3.refs_3_
  33.3 0.9 copy-done.1
  34.2 0.3 copy-done.2
  34.4 0.3 copy-done.3
  34.7 5.5 %factor_slices.1 = (f32[3,16,1024]{2,1,0:T(8,128)}, f32[3,16,1024]{2,1,0:T(8,128)}, f32[3,16,1024]{2,1,0:T(8,128)}, f32[3,16,1024]{2,1,0:T(8,128)}) custom-call(f32[3,64,1024]{2,1,0:T(8,128)} %get-tuple-element.32.refs_0_, f32[3,64,1024]{2,1,0:T(8,128)} %copy-done.1, f32[3,64,1024]{2,1,0:T(8,128)} %copy-done.2, f32[3,64,1024]{2,1,0:T(8,128)} %copy-done.3, ...), custom_call_target="tpu_custom_call" | custom-call | tf_op jit(solution)/shard_map/factor_slices/pallas_call | solution.py:132
  40.3 0.7 collective-permute-start.4
  40.9 1.3 collective-permute-start.5
  42.2 1.4 collective-permute-start.6
  43.6 0.0 collective-permute-done.4
  43.6 26.6 %collective-permute-done.5 = f32[3,16,1024]{2,1,0:T(8,128)S(1)} collective-permute-done((f32[3,16,1024]{2,1,0:T(8,128)}, f32[3,16,1024]{2,1,0:T(8,128)S(1)}, u32[]{:S(2)}, u32[]{:S(2)}) %collective-permute-start.5) | collective-permute-done | bytes 196640 | tf_op jit(solution)/shard_map/ppermute | solution.py:304
  70.2 1.6 add_select_fusion
  71.9 0.0 collective-permute-done.7
  71.9 0.0 all-gather.3.cloned.1.call-update
  71.9 6.2 %collective-permute-start.9 = (f32[3,16,1024]{2,1,0:T(8,128)}, f32[3,16,1024]{2,1,0:T(8,128)S(1)}, u32[]{:S(2)}, u32[]{:S(2)}) collective-permute-start(f32[3,16,1024]{2,1,0:T(8,128)} %add_select_fusion), channel_id=1, source_target_pairs={{0,0},{1,4},{2,8},{3,12},{4,1},{5,5},{6,9},{7,13},{8,2},{9,6},{10,... | collective-permute-start | bytes 589832 | tf_op jit(solution)/shard_map/ppermute | solution.py:319
  78.1 6.6 %collective-permute-start.10 = (f32[512,512]{1,0:T(8,128)}, f32[512,512]{1,0:T(8,128)}, u32[]{:S(2)}, u32[]{:S(2)}) collective-permute-start(f32[512,512]{1,0:T(8,128)} %get-tuple-element.49), channel_id=1, source_target_pairs={{0,0},{1,64},{2,128},{3,192},{4,4},{5,68},{6,132},{7,196},{9,72},{... | collective-permute-start | bytes 3145736 | tf_op jit(solution)/shard_map/ppermute | solution.py:289
  84.7 2.3 %collective-permute-start.11 = (f32[512,512]{1,0:T(8,128)}, f32[512,512]{1,0:T(8,128)}, u32[]{:S(2)}, u32[]{:S(2)}) collective-permute-start(f32[512,512]{1,0:T(8,128)} %get-tuple-element.50), channel_id=1, source_target_pairs={{0,1},{1,65},{2,129},{3,193},{4,5},{5,69},{6,133},{7,197},{8,9},{9... | collective-permute-start | bytes 3145736 | tf_op jit(solution)/shard_map/ppermute | solution.py:289
  87.0 1.6 collective-permute-start.12
  88.6 1.7 collective-permute-start.14
  90.3 8.7 %collective-permute-done.9 = f32[3,16,1024]{2,1,0:T(8,128)S(1)} collective-permute-done((f32[3,16,1024]{2,1,0:T(8,128)}, f32[3,16,1024]{2,1,0:T(8,128)S(1)}, u32[]{:S(2)}, u32[]{:S(2)}) %collective-permute-start.9) | collective-permute-done | bytes 196640 | tf_op jit(solution)/shard_map/ppermute | solution.py:319
  98.9 8.5 %collective-permute-start.13 = (f32[512,512]{1,0:T(8,128)}, f32[512,512]{1,0:T(8,128)}, u32[]{:S(2)}, u32[]{:S(2)}) collective-permute-start(f32[512,512]{1,0:T(8,128)} %get-tuple-element.54), channel_id=1, source_target_pairs={{1,67},{2,131},{3,195},{5,71},{6,135},{7,199},{9,75},{10,139},{11,... | collective-permute-start | bytes 3145736 | tf_op jit(solution)/shard_map/ppermute | solution.py:289
  107.4 1.2 slice.7
  109.3 2.4 %broadcast_select_fusion.2.early = f32[512,512]{1,0:T(8,128)} fusion(f32[512,512]{1,0:T(8,128)} %collective-permute-done.7, f32[512,512]{1,0:T(8,128)S(1)} %collective-permute-done.8, pred[]{:T(512)S(6)} %eq.12), kind=kLoop, calls=%fused_computation.2 | loop fusion | flops 262144 | bytes 3145729 | tf_op jit(solution)/shard_map/jit(_where)/select_n | solution.py:314
  111.7 41.0 %conditional.1 = (f32[16,3,16,1024]{3,2,1,0:T(8,128)S(1)}) conditional(s32[]{:T(128)} %bitcast.5, () %tuple.14, f32[3,16,1024]{2,1,0:T(8,128)S(1)} %collective-permute-done.9), branch_computations={%region_0.1_spmd, %region_1.2_spmd} | conditional | bytes 9633800 | solution.py:325
  111.7 0.4 broadcast_in_dim.2
  112.1 40.6 %all_to_all.4 = f32[16,3,16,1024]{3,2,1,0:T(8,128)S(1)} all-to-all(f32[16,3,16,1024]{3,2,1,0:T(8,128)S(1)} %broadcast_in_dim.2), channel_id=1, replica_groups=mesh['sub'=4,'row'=16,'col'=4] {'row'}, dimensions={0} | all-to-all | bytes 6291456 | tf_op jit(solution)/shard_map/cond/branch_1_fun/all_to_all | solution.py:323
  152.7 9.2 %update.1.partial = f32[768,768]{1,0:T(8,128)} custom-call(s32[3]{0:T(128)} %pad_add_fusion.ids, s32[4,32]{1,0:T(4,128)} %cmap.5, f32[768,768]{1,0:T(8,128)} %front.3, f32[512,512]{1,0:T(8,128)} %broadcast_select_fusion.2.early, f32[16,3,16,1024]{3,2,1,0:T(8,128)} %bitcast.6, f32[16,3,16,1024]{3,2,1,0:T(8,128)S(1)} %get-tuple-element.55.refs_1_), custom_call_target="tpu_custom_call" | custom-call | tf_op jit(solution)/shard_map/update/pallas_call | solution.py:202
  162.0 0.9 collective-permute-done.10.r0
  162.9 12.4 %collective-permute-done.11.r1 = f32[512,512]{1,0:T(8,128)} collective-permute-done((f32[512,512]{1,0:T(8,128)}, f32[512,512]{1,0:T(8,128)}, u32[]{:S(2)}, u32[]{:S(2)}) %collective-permute-start.11) | collective-permute-done | bytes 1048608 | tf_op jit(solution)/shard_map/ppermute | solution.py:289
  175.3 0.0 collective-permute-done.14.r4
  175.3 36.8 %collective-permute-done.13.r3 = f32[512,512]{1,0:T(8,128)} collective-permute-done((f32[512,512]{1,0:T(8,128)}, f32[512,512]{1,0:T(8,128)}, u32[]{:S(2)}, u32[]{:S(2)}) %collective-permute-start.13) | collective-permute-done | bytes 1048608 | tf_op jit(solution)/shard_map/ppermute | solution.py:289
  212.1 7.6 %finish.1 = f32[768,768]{1,0:T(8,128)} custom-call(s32[3]{0:T(128)} %pad_add_fusion.ids, s32[4,32]{1,0:T(4,128)} %cmap.5, f32[768,768]{1,0:T(8,128)} %update.1.partial, f32[512,512]{1,0:T(8,128)} %collective-permute-done.10.r0, f32[512,512]{1,0:T(8,128)} %collective-permute-done.11.r1, f32[512,512]{1,0:T(8,128)} %collective-permute-done.12.r2, ...), custom_call_target="tpu_custom_call" | custom-call | tf_op jit(solution)/shard_map/finish/pallas_call | solution.py:251
  (9 shorter events, 0.0 us)
Async XLA Ops:
  6.5 146.2 %all-gather.3.cloned.1.call-start = ((), (), s32[]{:S(2)}) async-start(), calls=%async_computation.1 | async-start | bytes 3342336 | tf_op jit(solution)/shard_map/all_gather | solution.py:328
  7.7 10.5 %collective-permute-start = (f32[768,256]{1,0:T(8,128)S(1)}, f32[768,256]{1,0:T(8,128)S(1)}, u32[]{:S(2)}, u32[]{:S(2)}) collective-permute-start(f32[768,256]{1,0:T(8,128)S(1)} %slice.6), channel_id=1, source_target_pairs={{1,0},{5,4},{9,8},{13,12},{17,16},{21,20},{25,24},{29,28},{33,32},... | collective-permute-start | bytes 2359304 | tf_op jit(solution)/shard_map/ppermute | solution.py:296
  14.9 57.0 %collective-permute-start.7 = (f32[512,512]{1,0:T(8,128)S(1)}, f32[512,512]{1,0:T(8,128)}, u32[]{:S(2)}, u32[]{:S(2)}) collective-permute-start(f32[512,512]{1,0:T(8,128)S(1)} %broadcast_select_fusion.1), channel_id=1, source_target_pairs={{0,2},{4,6},{8,10},{12,14},{16,18},{20,22},{24,26},{28,30},{32,34}... | collective-permute-start | bytes 3145736 | tf_op jit(solution)/shard_map/ppermute | solution.py:292
  18.2 0.9 copy-start
  23.4 9.8 %collective-permute-start.1 = (f32[3,64,1024]{2,1,0:T(8,128)}, f32[3,64,1024]{2,1,0:T(8,128)S(1)}, u32[]{:S(2)}, u32[]{:S(2)}) collective-permute-start(f32[3,64,1024]{2,1,0:T(8,128)} %get-tuple-element.33), channel_id=1, source_target_pairs={{0,64},{64,128},{128,192},{192,0},{4,68},{68,132},{132,196},{196,4... | collective-permute-start | bytes 2359304 | tf_op jit(solution)/shard_map/ppermute | solution.py:301
  24.1 9.1 %collective-permute-start.2 = (f32[3,64,1024]{2,1,0:T(8,128)}, f32[3,64,1024]{2,1,0:T(8,128)S(1)}, u32[]{:S(2)}, u32[]{:S(2)}) collective-permute-start(f32[3,64,1024]{2,1,0:T(8,128)} %get-tuple-element.34), channel_id=1, source_target_pairs={{0,128},{64,192},{128,0},{192,64},{4,132},{68,196},{132,4},{196,68... | collective-permute-start | bytes 2359304 | tf_op jit(solution)/shard_map/ppermute | solution.py:301
  24.9 8.4 %collective-permute-start.3 = (f32[3,64,1024]{2,1,0:T(8,128)}, f32[3,64,1024]{2,1,0:T(8,128)S(1)}, u32[]{:S(2)}, u32[]{:S(2)}) collective-permute-start(f32[3,64,1024]{2,1,0:T(8,128)} %get-tuple-element.35), channel_id=1, source_target_pairs={{0,192},{64,0},{128,64},{192,128},{4,196},{68,4},{132,68},{196,132... | collective-permute-start | bytes 2359304 | tf_op jit(solution)/shard_map/ppermute | solution.py:301
  27.0 44.9 %collective-permute-start.8 = (f32[512,512]{1,0:T(8,128)S(1)}, f32[512,512]{1,0:T(8,128)S(1)}, u32[]{:S(2)}, u32[]{:S(2)}) collective-permute-start(f32[512,512]{1,0:T(8,128)S(1)} %broadcast_select_fusion), channel_id=1, source_target_pairs={{0,3},{4,7},{8,11},{12,15},{16,19},{20,23},{24,27},{28,31},{32,35}... | collective-permute-start | bytes 3145736 | tf_op jit(solution)/shard_map/ppermute | solution.py:292
  33.3 0.9 copy-start.1
  33.3 1.1 copy-start.2
  33.3 1.5 copy-start.3
  40.3 3.3 %collective-permute-start.4 = (f32[3,16,1024]{2,1,0:T(8,128)}, f32[3,16,1024]{2,1,0:T(8,128)S(1)}, u32[]{:S(2)}, u32[]{:S(2)}) collective-permute-start(f32[3,16,1024]{2,1,0:T(8,128)} %get-tuple-element.39), channel_id=1, source_target_pairs={{0,1},{64,65},{128,129},{192,193},{4,5},{68,69},{132,133},{196,197... | collective-permute-start | bytes 589832 | tf_op jit(solution)/shard_map/ppermute | solution.py:304
  40.9 29.3 %collective-permute-start.5 = (f32[3,16,1024]{2,1,0:T(8,128)}, f32[3,16,1024]{2,1,0:T(8,128)S(1)}, u32[]{:S(2)}, u32[]{:S(2)}) collective-permute-start(f32[3,16,1024]{2,1,0:T(8,128)} %get-tuple-element.40), channel_id=1, source_target_pairs={{0,2},{64,66},{128,130},{192,194},{4,6},{68,70},{132,134},{196,198... | collective-permute-start | bytes 589832 | tf_op jit(solution)/shard_map/ppermute | solution.py:304
  42.2 28.0 %collective-permute-start.6 = (f32[3,16,1024]{2,1,0:T(8,128)}, f32[3,16,1024]{2,1,0:T(8,128)}, u32[]{:S(2)}, u32[]{:S(2)}) collective-permute-start(f32[3,16,1024]{2,1,0:T(8,128)} %get-tuple-element.41), channel_id=1, source_target_pairs={{0,3},{64,67},{128,131},{192,195},{4,7},{68,71},{132,135},{196,199... | collective-permute-start | bytes 589832 | tf_op jit(solution)/shard_map/ppermute | solution.py:304
  71.9 27.0 %collective-permute-start.9 = (f32[3,16,1024]{2,1,0:T(8,128)}, f32[3,16,1024]{2,1,0:T(8,128)S(1)}, u32[]{:S(2)}, u32[]{:S(2)}) collective-permute-start(f32[3,16,1024]{2,1,0:T(8,128)} %add_select_fusion), channel_id=1, source_target_pairs={{0,0},{1,4},{2,8},{3,12},{4,1},{5,5},{6,9},{7,13},{8,2},{9,6},{10,... | collective-permute-start | bytes 589832 | tf_op jit(solution)/shard_map/ppermute | solution.py:319
  78.1 84.8 %collective-permute-start.10 = (f32[512,512]{1,0:T(8,128)}, f32[512,512]{1,0:T(8,128)}, u32[]{:S(2)}, u32[]{:S(2)}) collective-permute-start(f32[512,512]{1,0:T(8,128)} %get-tuple-element.49), channel_id=1, source_target_pairs={{0,0},{1,64},{2,128},{3,192},{4,4},{5,68},{6,132},{7,196},{9,72},{... | collective-permute-start | bytes 3145736 | tf_op jit(solution)/shard_map/ppermute | solution.py:289
  84.7 90.6 %collective-permute-start.11 = (f32[512,512]{1,0:T(8,128)}, f32[512,512]{1,0:T(8,128)}, u32[]{:S(2)}, u32[]{:S(2)}) collective-permute-start(f32[512,512]{1,0:T(8,128)} %get-tuple-element.50), channel_id=1, source_target_pairs={{0,1},{1,65},{2,129},{3,193},{4,5},{5,69},{6,133},{7,197},{8,9},{9... | collective-permute-start | bytes 3145736 | tf_op jit(solution)/shard_map/ppermute | solution.py:289
  87.0 88.3 %collective-permute-start.12 = (f32[512,512]{1,0:T(8,128)}, f32[512,512]{1,0:T(8,128)}, u32[]{:S(2)}, u32[]{:S(2)}) collective-permute-start(f32[512,512]{1,0:T(8,128)} %get-tuple-element.51), channel_id=1, source_target_pairs={{1,66},{3,194},{5,70},{7,198},{9,74},{11,202},{13,78},{15,206},{17... | collective-permute-start | bytes 3145736 | tf_op jit(solution)/shard_map/ppermute | solution.py:289
  88.6 86.7 %collective-permute-start.14 = (f32[512,512]{1,0:T(8,128)}, f32[512,512]{1,0:T(8,128)}, u32[]{:S(2)}, u32[]{:S(2)}) collective-permute-start(f32[512,512]{1,0:T(8,128)} %collective-permute-done.7), channel_id=1, source_target_pairs={{65,130},{69,134},{73,138},{77,142},{81,146},{85,150},{89,154},{93... | collective-permute-start | bytes 3145736 | tf_op jit(solution)/shard_map/ppermute | solution.py:310
  98.9 113.2 %collective-permute-start.13 = (f32[512,512]{1,0:T(8,128)}, f32[512,512]{1,0:T(8,128)}, u32[]{:S(2)}, u32[]{:S(2)}) collective-permute-start(f32[512,512]{1,0:T(8,128)} %get-tuple-element.54), channel_id=1, source_target_pairs={{1,67},{2,131},{3,195},{5,71},{6,135},{7,199},{9,75},{10,139},{11,... | collective-permute-start | bytes 3145736 | tf_op jit(solution)/shard_map/ppermute | solution.py:289
Sparse Core Ops, SparseCore 0:
  72.0 67.3 all-gather.2
